TPU v7x, 128 devices: a whole 4x4x4 slice. The times are simulated.
128 devices in a mesh: segment: 8 (over x, core), strip: 16 (over z, y).
Axes of the slice: x: 4, y: 4, z: 4, core: 2. Of those that a mesh axis runs over, the one named last changes fastest.
Arguments:
- held_blocks: bfloat16 [8, 4, 128, 12, 384], P('segment', None, 'strip'), may hold values from -6 to 6
- incoming: bfloat16 [1, 4, 128, 12, 384], P(None, None, 'strip'), may hold values from -6 to 6
- frame_counts: int32 [9], replicated, may hold values from 1 to 4, as said below
- first_cache: bfloat16 [8, 2, 128, 12, 384], P('segment', None, 'strip'), may hold values from -0.25 to 2
- second_cache: bfloat16 [8, 2, 128, 12, 384], P('segment', None, 'strip'), may hold values from -0.25 to 2
- first_kernel: bfloat16 [8, 3, 3, 3, 384, 384], P('segment'), may hold values from -0.0625 to 0.0625
- first_bias: float32 [8, 384], P('segment'), may hold values from -3 to 3
- first_gain: float32 [8, 384], P('segment'), may hold values from 0.5 to 2
- second_kernel: bfloat16 [8, 3, 3, 3, 384, 384], P('segment'), may hold values from -0.0625 to 0.0625
- second_bias: float32 [8, 384], P('segment'), may hold values from -3 to 3
- second_gain: float32 [8, 384], P('segment'), may hold values from 0.5 to 2
Outputs:
- section_out: bfloat16 [2, 8, 4, 128, 12, 384], P(None, 'segment', None, 'strip')
- first_cache_out: bfloat16 [8, 2, 128, 12, 384], P('segment', None, 'strip')
- second_cache_out: bfloat16 [8, 2, 128, 12, 384], P('segment', None, 'strip')
Inputs may be any that keep to these rules, and one draw needn't show every extreme that they name: `frame_counts`: the section at segment index s works at tick t (from 0) on block 7 - s + t; both 1 and 4 occur in every draw.
All inputs are finite; a program needn't handle non-finite values.
Results may differ from a plain program's by a relative error of at most 0.0051.
Values may be sent and summed in bfloat16 or wider, within the bound.
No kernel may reach another device: no remote copies, remote signals or barrier semaphores. Data moves between devices by JAX's collectives and lax.ppermute only.
A program may use at most 128 MiB of HBM per device.

v0:
```python
import jax
import jax.numpy as jnp
from jax import lax
from jax.experimental import pallas as pl
from jax.experimental.pallas import tpu as pltpu
from jax.sharding import PartitionSpec as P

EPSILON = 1e-06
C = 384
FRAMES = 4
COLS = 12
ROWS = 8
MAIN = COLS * ROWS
EDGE = COLS * 2
BLOCK = 128
TAPS = 9
K = TAPS * C
BF16 = jnp.bfloat16
F32 = jnp.float32
VMEM = pl.BlockSpec(memory_space=pltpu.VMEM)
SMEM = pl.BlockSpec(memory_space=pltpu.SMEM)
ANY = pl.BlockSpec(memory_space=pl.ANY)


def rolled(value, shift, axis):
    shift = shift % value.shape[axis]
    return pltpu.roll(value, shift, axis) if shift else value


def rows_out(main, first):
    split = main.reshape(3, 4, ROWS, C)
    group = lax.broadcasted_iota(jnp.int32, (3, ROWS, C), 1) // 2
    out = None
    for q in range(4):
        piece = rolled(split[:, q], 2 * q - first, 1)
        out = piece if out is None else jnp.where(group == q, piece, out)
    return out.reshape(EDGE, C)


def spread(edge, which, to):
    split = edge.reshape(3, ROWS, C)
    pieces = [rolled(split, to - (2 * q + which), 1) for q in range(4)]
    return jnp.stack(pieces, axis=1).reshape(COLS, ROWS, C)


def shifted_rows(main, before, before_which, after, after_which):
    split = main.reshape(COLS, ROWS, C)
    place = lax.broadcasted_iota(jnp.int32, (COLS, ROWS, C), 1)
    down = jnp.where(place == 0, spread(before, before_which, 0), rolled(split, 1, 1))
    up = jnp.where(place == ROWS - 1, spread(after, after_which, ROWS - 1), rolled(split, -1, 1))
    return [down.reshape(MAIN, C), main, up.reshape(MAIN, C)]


def column_taps(main):
    zeros = jnp.zeros((ROWS, C), F32)
    return [
        jnp.concatenate([zeros, main[: MAIN - ROWS]], axis=0),
        main,
        jnp.concatenate([main[ROWS:], zeros], axis=0),
    ]


def edge_column_taps(edge):
    place = lax.broadcasted_iota(jnp.int32, (EDGE, C), 0)
    return [
        jnp.where(place < 2, 0.0, rolled(edge, 2, 0)),
        edge,
        jnp.where(place >= EDGE - 2, 0.0, rolled(edge, -2, 0)),
    ]


def edge_pair(top, bottom):
    even = lax.broadcasted_iota(jnp.int32, (EDGE, C), 0) % 2 == 0
    return jnp.where(even, rolled(top, -1, 0), rolled(bottom, 1, 0))


def normed(values, gain):
    factor = lax.rsqrt(jnp.mean(values * values, axis=-1, keepdims=True) + EPSILON)
    v = values * factor * gain
    return v / (1.0 + jnp.exp(-v))


def build_first(window, operand, frame):
    main = window[frame, 0:MAIN].astype(F32)
    halo = window[frame, MAIN : MAIN + 2 * EDGE].astype(F32)
    top, bottom = halo[:EDGE], halo[EDGE:]
    even = lax.broadcasted_iota(jnp.int32, (EDGE, C), 0) % 2 == 0
    mains = shifted_rows(main, top, 1, bottom, 0)
    edges = [
        jnp.where(even, top, rows_out(main, 6)),
        edge_pair(top, bottom),
        jnp.where(even, rows_out(main, 0), bottom),
    ]
    zeros = jnp.zeros((BLOCK - MAIN - EDGE, C), F32)
    for b in range(3):
        for c, (m, e) in enumerate(zip(column_taps(mains[b]), edge_column_taps(edges[b]))):
            at = (3 * b + c) * C
            operand[frame, :, at : at + C] = jnp.concatenate([m, e, zeros], axis=0).astype(BF16)


def build_second(window, operand, frame):
    main = window[frame, 0:MAIN].astype(F32)
    edge = window[frame, MAIN:BLOCK].astype(F32)[:EDGE]
    mains = shifted_rows(main, edge, 0, edge, 1)
    for b in range(3):
        for c, m in enumerate(column_taps(mains[b])):
            at = (3 * b + c) * C
            operand[frame, :, at : at + C] = m.astype(BF16)


def pack_kernel(x, first, second, up, down):
    for source, start in ((x, 0), (first, 4), (second, 6)):
        for f in range(source.shape[0]):
            main = source[f].astype(F32)
            up[start + f] = rows_out(main, 0).astype(BF16)
            down[start + f] = rows_out(main, 6).astype(BF16)


def tick_kernel(tick, *refs):
    if tick == 0:
        (counts, x, tops, bottoms, first_cache, second_cache, incoming, first_w, first_bias, first_gain, second_w,
         second_bias, second_gain, out, send, send_up, send_down, first_next, first_halo, second_next, second_edge,
         *scratch) = refs
    else:
        (counts, x, tops, bottoms, first_cache, first_cache_halo, second_cache, second_cache_edge, first_w, first_bias,
         first_gain, second_w, second_bias, second_gain, out, first_next, second_next, *scratch) = refs
    window1, window2, operand1, operand2, sums1, sums2, weights1, weights2, sems = scratch
    copies = []
    for i in range(3):
        copies.append(pltpu.make_async_copy(first_w.at[i], weights1.at[i], sems.at[i]))
    for i in range(3):
        copies.append(pltpu.make_async_copy(second_w.at[i], weights2.at[i], sems.at[3 + i]))
    for copy in copies:
        copy.start()
    segment = lax.axis_index("segment")
    strip = lax.axis_index("strip")
    live = counts[7 - segment + tick]

    window1[0:2, 0:MAIN] = first_cache[...]
    if tick == 0:
        window1[0:2, MAIN : MAIN + EDGE] = tops[4:6]
        window1[0:2, MAIN + EDGE : MAIN + 2 * EDGE] = bottoms[4:6]
    else:
        window1[0:2, MAIN : MAIN + 2 * EDGE] = first_cache_halo[...]
    gain1 = first_gain[...]

    @pl.loop(0, FRAMES)
    def _(f):
        keep = f < live
        for source, at, length in ((x, 0, MAIN), (tops, MAIN, EDGE), (bottoms, MAIN + EDGE, EDGE)):
            values = jnp.where(keep, source[f].astype(F32), 0.0)
            window1[f + 2, at : at + length] = normed(values, gain1).astype(BF16)

    @pl.loop(0, FRAMES + 2)
    def _(g):
        build_first(window1, operand1, g)

    for a in range(3):
        copies[a].wait()
        lhs = operand1[a : a + FRAMES].reshape(FRAMES * BLOCK, K)
        product = jnp.dot(lhs, weights1[a], preferred_element_type=F32)
        if a == 0:
            sums1[...] = product
        else:
            sums1[...] += product

    window2[0:2, 0:MAIN] = second_cache[...]
    if tick == 0:
        for f in range(2):
            edge = edge_pair(tops[6 + f].astype(F32), bottoms[6 + f].astype(F32))
            window2[f, MAIN : MAIN + EDGE] = edge.astype(BF16)
    else:
        window2[0:2, MAIN : MAIN + EDGE] = second_cache_edge[...]
    gain2 = second_gain[...]
    bias1 = first_bias[...]
    place = lax.broadcasted_iota(jnp.int32, (BLOCK, C), 0)
    outside = (place >= MAIN) & (
        ((place % 2 == 0) & (strip == 0)) | ((place % 2 == 1) & (strip == lax.axis_size("strip") - 1))
    )

    @pl.loop(0, FRAMES)
    def _(f):
        at = pl.multiple_of(f * BLOCK, BLOCK)
        hidden = sums1[pl.ds(at, BLOCK)] + bias1
        hidden = jnp.where(outside | (f >= live), 0.0, hidden)
        window2[f + 2] = normed(hidden, gain2).astype(BF16)

    @pl.loop(0, FRAMES + 2)
    def _(g):
        build_second(window2, operand2, g)

    for a in range(3):
        copies[3 + a].wait()
        lhs = operand2[a : a + FRAMES].reshape(FRAMES * MAIN, K)
        product = jnp.dot(lhs, weights2[a], preferred_element_type=F32)
        if a == 0:
            sums2[...] = product
        else:
            sums2[...] += product
    bias2 = second_bias[...]

    @pl.loop(0, FRAMES)
    def _(f):
        at = pl.multiple_of(f * MAIN, MAIN)
        keep = f < live
        result = sums2[pl.ds(at, MAIN)] + bias2 + x[f].astype(F32)
        result = jnp.where(keep, result, 0.0).astype(BF16)
        out[f] = result
        if tick == 0:
            passed = jnp.where(segment == lax.axis_size("segment") - 1, incoming[f].astype(F32), result.astype(F32))
            send[f] = passed.astype(BF16)
            send_up[f] = rows_out(passed, 0).astype(BF16)
            send_down[f] = rows_out(passed, 6).astype(BF16)

    for i in range(2):
        first_next[i] = window1[live + i, 0:MAIN]
        second_next[i] = window2[live + i, 0:MAIN]
        if tick == 0:
            first_halo[i] = window1[live + i, MAIN : MAIN + 2 * EDGE]
            second_edge[i] = window2[live + i, MAIN : MAIN + EDGE]


def shape(*dims):
    return jax.ShapeDtypeStruct(dims, BF16)


def run_tick(tick, operands, out_shapes):
    places = [VMEM] * len(operands)
    places[0] = SMEM
    for i in (-6, -3):
        places[i] = ANY
    return pl.pallas_call(
        lambda *refs: tick_kernel(tick, *refs),
        out_shape=out_shapes,
        in_specs=places,
        out_specs=[VMEM] * len(out_shapes),
        scratch_shapes=[
            pltpu.VMEM((FRAMES + 2, MAIN + 2 * EDGE, C), BF16),
            pltpu.VMEM((FRAMES + 2, BLOCK, C), BF16),
            pltpu.VMEM((FRAMES + 2, BLOCK, K), BF16),
            pltpu.VMEM((FRAMES + 2, MAIN, K), BF16),
            pltpu.VMEM((FRAMES * BLOCK, C), F32),
            pltpu.VMEM((FRAMES * MAIN, C), F32),
            pltpu.VMEM((3, K, C), BF16),
            pltpu.VMEM((3, K, C), BF16),
            pltpu.SemaphoreType.DMA((6,)),
        ],
        compiler_params=pltpu.CompilerParams(vmem_limit_bytes=56 << 20),
        name=f"tick{tick}",
    )(*operands)


def flat(array):
    frames = array.shape[0]
    return array.transpose(0, 2, 1, 3).reshape(frames, MAIN, C)


def unflat(array):
    frames = array.shape[0]
    return array.reshape(frames, COLS, ROWS, C).transpose(0, 2, 1, 3)


def on_device(
    held_blocks,
    incoming,
    frame_counts,
    first_cache,
    second_cache,
    first_kernel,
    first_bias,
    first_gain,
    second_kernel,
    second_bias,
    second_gain,
):
    segments = lax.axis_size("segment")
    strips = lax.axis_size("strip")
    x = flat(held_blocks[0])
    fresh = flat(incoming[0])
    first = flat(first_cache[0])
    second = flat(second_cache[0])
    params = (
        first_kernel[0].reshape(3, K, C),
        first_bias,
        first_gain,
        second_kernel[0].reshape(3, K, C),
        second_bias,
        second_gain,
    )
    up, down = pl.pallas_call(
        pack_kernel, out_shape=[shape(8, EDGE, C)] * 2, in_specs=[VMEM] * 3, out_specs=[VMEM] * 2, name="pack"
    )(x, first, second)
    forward = [(i, i + 1) for i in range(strips - 1)]
    backward = [(j, i) for i, j in forward]
    tops = lax.ppermute(down, "strip", forward)
    bottoms = lax.ppermute(up, "strip", backward)
    out0, send, send_up, send_down, first, first_halo, second, second_edge = run_tick(
        0,
        (frame_counts, x, tops, bottoms, first, second, fresh, *params),
        [shape(FRAMES, MAIN, C)] * 2
        + [shape(FRAMES, EDGE, C)] * 2
        + [shape(2, MAIN, C), shape(2, 2 * EDGE, C), shape(2, MAIN, C), shape(2, EDGE, C)],
    )

    def pairs(step):
        return [
            (s * strips + k, (s + 1) % segments * strips + k + step)
            for s in range(segments)
            for k in range(strips)
            if 0 <= k + step < strips
        ]

    axes = ("segment", "strip")
    tops = lax.ppermute(send_down, axes, pairs(1))
    bottoms = lax.ppermute(send_up, axes, pairs(-1))
    x = lax.ppermute(send, axes, pairs(0))
    out1, first, second = run_tick(
        1,
        (frame_counts, x, tops, bottoms, first, first_halo, second, second_edge, *params),
        [shape(FRAMES, MAIN, C), shape(2, MAIN, C), shape(2, MAIN, C)],
    )
    return (
        jnp.stack([unflat(out0), unflat(out1)])[:, None],
        unflat(first)[None],
        unflat(second)[None],
    )


def solution(mesh):
    return jax.shard_map(
        on_device,
        mesh=mesh,
        in_specs=(
            P("segment", None, "strip", None, None),
            P(None, None, "strip", None, None),
            P(),
            P("segment", None, "strip", None, None),
            P("segment", None, "strip", None, None),
            P("segment", None, None, None, None, None),
            P("segment", None),
            P("segment", None),
            P("segment", None, None, None, None, None),
            P("segment", None),
            P("segment", None),
        ),
        out_specs=(
            P(None, "segment", None, "strip", None, None),
            P("segment", None, "strip", None, None),
            P("segment", None, "strip", None, None),
        ),
        check_vma=False,
    )
```

profile of v0, /device:TPU:24, one launch (start us, length us, event | category | flops | bytes accessed | tf_op | source)
XLA Modules:
  0.0 64.1 jit_solution(15922730661168729020)
XLA Ops:
  0.6 1.9 %pack.1 = (bf16[8,24,384]{2,1,0:T(8,128)(2,1)}, bf16[8,24,384]{2,1,0:T(8,128)(2,1)}) custom-call(bf16[4,96,384]{2,1,0:T(8,128)(2,1)} %bitcast.48, bf16[2,96,384]{2,1,0:T(8,128)(2,1)} %bitcast.50, bf16[2,96,384]{2,1,0:T(8,128)(2,1)} %bitcast.52), custom_call_target="tpu_custom_call" | custom-call | tf_op jit(solution)/shard_map/pack/pallas_call | solution.py:290
  2.6 3.5 %collective-permute-start = (bf16[8,24,384]{2,1,0:T(8,128)(2,1)}, bf16[8,24,384]{2,1,0:T(8,128)(2,1)S(1)}, u32[]{:S(2)}, u32[]{:S(2)}) collective-permute-start(bf16[8,24,384]{2,1,0:T(8,128)(2,1)} %get-tuple-element.16), channel_id=1, source_target_pairs={{0,1},{1,2},{2,3},{3,4},{4,5},{5,6},{6,7},{7,8},{8,9},{9,10},{10,1... | collective-permute-start | bytes 442376 | tf_op jit(solution)/shard_map/ppermute | solution.py:295
  6.1 2.4 %collective-permute-start.1 = (bf16[8,24,384]{2,1,0:T(8,128)(2,1)}, bf16[8,24,384]{2,1,0:T(8,128)(2,1)S(1)}, u32[]{:S(2)}, u32[]{:S(2)}) collective-permute-start(bf16[8,24,384]{2,1,0:T(8,128)(2,1)} %get-tuple-element.17), channel_id=1, source_target_pairs={{1,0},{2,1},{3,2},{4,3},{5,4},{6,5},{7,6},{8,7},{9,8},{10,9},{11,1... | collective-permute-start | bytes 442376 | tf_op jit(solution)/shard_map/ppermute | solution.py:296
  8.4 1.8 %collective-permute-done.refs_2_ = bf16[8,24,384]{2,1,0:T(8,128)(2,1)S(1)} collective-permute-done((bf16[8,24,384]{2,1,0:T(8,128)(2,1)}, bf16[8,24,384]{2,1,0:T(8,128)(2,1)S(1)}, u32[]{:S(2)}, u32[]{:S(2)}) %collective-permute-start) | collective-permute-done | bytes 147488 | tf_op jit(solution)/shard_map/ppermute | solution.py:295
  10.3 0.0 copy-start.2
  10.3 5.3 %collective-permute-done.1.refs_3_ = bf16[8,24,384]{2,1,0:T(8,128)(2,1)S(1)} collective-permute-done((bf16[8,24,384]{2,1,0:T(8,128)(2,1)}, bf16[8,24,384]{2,1,0:T(8,128)(2,1)S(1)}, u32[]{:S(2)}, u32[]{:S(2)}) %collective-permute-start.1) | collective-permute-done | bytes 147488 | tf_op jit(solution)/shard_map/ppermute | solution.py:296
  15.6 0.0 copy-start.3
  15.6 0.0 copy-done.2
  15.6 0.7 %copy-done.3 = bf16[8,24,384]{2,1,0:T(8,128)(2,1)} copy-done((bf16[8,24,384]{2,1,0:T(8,128)(2,1)}, bf16[8,24,384]{2,1,0:T(8,128)(2,1)S(1)}, u32[]{:S(2)}) %copy-start.3) | copy-done | bytes 147480
  16.2 16.3 %tick0.1 = (bf16[4,96,384]{2,1,0:T(8,128)(2,1)}, bf16[4,96,384]{2,1,0:T(8,128)(2,1)}, bf16[4,24,384]{2,1,0:T(8,128)(2,1)}, bf16[4,24,384]{2,1,0:T(8,128)(2,1)}, ...) custom-call(s32[9]{0:T(128)} %refs_0_.3, ...), custom_call_target="tpu_custom_call" | custom-call | tf_op jit(solution)/shard_map/tick0/pallas_call | solution.py:232
  32.6 0.0 collective-permute-start.2
  32.6 2.7 %collective-permute-start.3 = (bf16[4,24,384]{2,1,0:T(8,128)(2,1)}, bf16[4,24,384]{2,1,0:T(8,128)(2,1)S(1)}, u32[]{:S(2)}, u32[]{:S(2)}) collective-permute-start(bf16[4,24,384]{2,1,0:T(8,128)(2,1)} %get-tuple-element.20), channel_id=1, source_target_pairs={{0,17},{1,18},{2,19},{3,20},{4,21},{5,22},{6,23},{7,24},{8,25},{9,... | collective-permute-start | bytes 221192 | tf_op jit(solution)/shard_map/ppermute | solution.py:314
  35.4 3.9 %collective-permute-start.4 = (bf16[4,24,384]{2,1,0:T(8,128)(2,1)}, bf16[4,24,384]{2,1,0:T(8,128)(2,1)S(1)}, u32[]{:S(2)}, u32[]{:S(2)}) collective-permute-start(bf16[4,24,384]{2,1,0:T(8,128)(2,1)} %get-tuple-element.21), channel_id=1, source_target_pairs={{1,16},{2,17},{3,18},{4,19},{5,20},{6,21},{7,22},{8,23},{9,24},{10... | collective-permute-start | bytes 221192 | tf_op jit(solution)/shard_map/ppermute | solution.py:315
  39.3 1.4 %collective-permute-done.3.refs_2_ = bf16[4,24,384]{2,1,0:T(8,128)(2,1)S(1)} collective-permute-done((bf16[4,24,384]{2,1,0:T(8,128)(2,1)}, bf16[4,24,384]{2,1,0:T(8,128)(2,1)S(1)}, u32[]{:S(2)}, u32[]{:S(2)}) %collective-permute-start.3) | collective-permute-done | bytes 73760 | tf_op jit(solution)/shard_map/ppermute | solution.py:314
  40.7 0.0 copy-start.4
  40.7 4.8 %collective-permute-done.4.refs_3_ = bf16[4,24,384]{2,1,0:T(8,128)(2,1)S(1)} collective-permute-done((bf16[4,24,384]{2,1,0:T(8,128)(2,1)}, bf16[4,24,384]{2,1,0:T(8,128)(2,1)S(1)}, u32[]{:S(2)}, u32[]{:S(2)}) %collective-permute-start.4) | collective-permute-done | bytes 73760 | tf_op jit(solution)/shard_map/ppermute | solution.py:315
  45.5 0.0 copy-start.5
  45.5 0.0 collective-permute-done.2.refs_1_
  45.5 0.0 copy-start.1
  45.5 0.0 copy-done.4
  45.5 0.6 copy-done.5
  46.1 0.1 copy-done.1
  46.2 0.0 copy-start
  46.2 16.0 %tick1.1 = (bf16[4,96,384]{2,1,0:T(8,128)(2,1)}, bf16[2,96,384]{2,1,0:T(8,128)(2,1)}, bf16[2,96,384]{2,1,0:T(8,128)(2,1)}) custom-call(s32[9]{0:T(128)} %refs_0_.3, bf16[4,96,384]{2,1,0:T(8,128)(2,1)} %copy-done.1, bf16[4,24,384]{2,1,0:T(8,128)(2,1)} %copy-done.4, bf16[4,24,384]{2,1,0:T(8,128)(2,1)} %copy-done.5, ...), custom_call_target="tpu_custom_call" | custom-call | tf_op jit(solution)/shard_map/tick1/pallas_call | solution.py:232
  62.2 0.0 copy-done
  62.2 1.8 %maximum_bitcast_fusion = bf16[2,1,4,8,12,384]{5,3,4,2,1,0:T(8,128)(2,1)} fusion(bf16[1,4,8,12,384]{4,2,3,1,0:T(8,128)(2,1)} %bitcast.55, bf16[1,4,8,12,384]{4,2,3,1,0:T(8,128)(2,1)S(1)} %bitcast.54), kind=kLoop, calls=%fused_computation | loop fusion | flops 294912 | bytes 1179648 | tf_op jit(solution)/shard_map/broadcast_in_dim | solution.py:323
Async XLA Ops:
  2.6 7.7 %collective-permute-start = (bf16[8,24,384]{2,1,0:T(8,128)(2,1)}, bf16[8,24,384]{2,1,0:T(8,128)(2,1)S(1)}, u32[]{:S(2)}, u32[]{:S(2)}) collective-permute-start(bf16[8,24,384]{2,1,0:T(8,128)(2,1)} %get-tuple-element.16), channel_id=1, source_target_pairs={{0,1},{1,2},{2,3},{3,4},{4,5},{5,6},{6,7},{7,8},{8,9},{9,10},{10,1... | collective-permute-start | bytes 442376 | tf_op jit(solution)/shard_map/ppermute | solution.py:295
  6.1 9.5 %collective-permute-start.1 = (bf16[8,24,384]{2,1,0:T(8,128)(2,1)}, bf16[8,24,384]{2,1,0:T(8,128)(2,1)S(1)}, u32[]{:S(2)}, u32[]{:S(2)}) collective-permute-start(bf16[8,24,384]{2,1,0:T(8,128)(2,1)} %get-tuple-element.17), channel_id=1, source_target_pairs={{1,0},{2,1},{3,2},{4,3},{5,4},{6,5},{7,6},{8,7},{9,8},{10,9},{11,1... | collective-permute-start | bytes 442376 | tf_op jit(solution)/shard_map/ppermute | solution.py:296
  10.3 5.3 %copy-start.2 = (bf16[8,24,384]{2,1,0:T(8,128)(2,1)}, bf16[8,24,384]{2,1,0:T(8,128)(2,1)S(1)}, u32[]{:S(2)}) copy-start(bf16[8,24,384]{2,1,0:T(8,128)(2,1)S(1)} %collective-permute-done.refs_2_) | copy-start | bytes 442372
  15.6 0.7 %copy-start.3 = (bf16[8,24,384]{2,1,0:T(8,128)(2,1)}, bf16[8,24,384]{2,1,0:T(8,128)(2,1)S(1)}, u32[]{:S(2)}) copy-start(bf16[8,24,384]{2,1,0:T(8,128)(2,1)S(1)} %collective-permute-done.1.refs_3_) | copy-start | bytes 442372
  32.6 12.9 %collective-permute-start.2 = (bf16[4,96,384]{2,1,0:T(8,128)(2,1)}, bf16[4,96,384]{2,1,0:T(8,128)(2,1)S(1)}, u32[]{:S(2)}, u32[]{:S(2)}) collective-permute-start(bf16[4,96,384]{2,1,0:T(8,128)(2,1)} %get-tuple-element.19), channel_id=1, source_target_pairs={{0,16},{1,17},{2,18},{3,19},{4,20},{5,21},{6,22},{7,23},{8,24},{9,... | collective-permute-start | bytes 884744 | tf_op jit(solution)/shard_map/ppermute | solution.py:316
  32.6 8.1 %collective-permute-start.3 = (bf16[4,24,384]{2,1,0:T(8,128)(2,1)}, bf16[4,24,384]{2,1,0:T(8,128)(2,1)S(1)}, u32[]{:S(2)}, u32[]{:S(2)}) collective-permute-start(bf16[4,24,384]{2,1,0:T(8,128)(2,1)} %get-tuple-element.20), channel_id=1, source_target_pairs={{0,17},{1,18},{2,19},{3,20},{4,21},{5,22},{6,23},{7,24},{8,25},{9,... | collective-permute-start | bytes 221192 | tf_op jit(solution)/shard_map/ppermute | solution.py:314
  35.4 10.1 %collective-permute-start.4 = (bf16[4,24,384]{2,1,0:T(8,128)(2,1)}, bf16[4,24,384]{2,1,0:T(8,128)(2,1)S(1)}, u32[]{:S(2)}, u32[]{:S(2)}) collective-permute-start(bf16[4,24,384]{2,1,0:T(8,128)(2,1)} %get-tuple-element.21), channel_id=1, source_target_pairs={{1,16},{2,17},{3,18},{4,19},{5,20},{6,21},{7,22},{8,23},{9,24},{10... | collective-permute-start | bytes 221192 | tf_op jit(solution)/shard_map/ppermute | solution.py:315
  40.7 4.8 %copy-start.4 = (bf16[4,24,384]{2,1,0:T(8,128)(2,1)}, bf16[4,24,384]{2,1,0:T(8,128)(2,1)S(1)}, u32[]{:S(2)}) copy-start(bf16[4,24,384]{2,1,0:T(8,128)(2,1)S(1)} %collective-permute-done.3.refs_2_) | copy-start | bytes 221188
  45.5 0.6 copy-start.5
  45.5 0.7 %copy-start.1 = (bf16[4,96,384]{2,1,0:T(8,128)(2,1)}, bf16[4,96,384]{2,1,0:T(8,128)(2,1)S(1)}, u32[]{:S(2)}) copy-start(bf16[4,96,384]{2,1,0:T(8,128)(2,1)S(1)} %collective-permute-done.2.refs_1_) | copy-start | bytes 884740
  46.2 16.0 %copy-start = (bf16[4,96,384]{2,1,0:T(8,128)(2,1)S(1)}, bf16[4,96,384]{2,1,0:T(8,128)(2,1)}, u32[]{:S(2)}) copy-start(bf16[4,96,384]{2,1,0:T(8,128)(2,1)} %get-tuple-element.18) | copy-start | bytes 884740
where the time goes:
time: 64.4 us; the launch traced here: 64.1 us
  Pallas kernels  34.3 us (53%)
  waiting for transfers between devices  13.3 us (21%)
  starting transfers between devices  12.5 us (19%)
  other arithmetic  1.84 us (3%)
  local copies, waits for them, and re-layouts  1.39 us (2%)
  between operations  0.71 us (1%)
    pallas_call x2, Pallas kernels, run_tick(): pl.pallas_call(lambda *refs: tick_kernel(tick, *refs), out_shape=out_shap...  32.3 us
    ppermute x1, waiting for transfers between devices, on_device(): bottoms = lax.ppermute(up, 'strip', backward)  5.32 us
    ppermute x1, waiting for transfers between devices, on_device(): bottoms = lax.ppermute(send_up, axes, pairs(-1))  4.76 us
    ppermute x1, starting transfers between devices, on_device(): bottoms = lax.ppermute(send_up, axes, pairs(-1))  3.92 us
    ppermute x1, starting transfers between devices, on_device(): tops = lax.ppermute(down, 'strip', forward)  3.47 us
    ppermute x1, starting transfers between devices, on_device(): tops = lax.ppermute(send_down, axes, pairs(1))  2.75 us
    ppermute x1, starting transfers between devices, on_device(): bottoms = lax.ppermute(up, 'strip', backward)  2.36 us
    pallas_call x1, Pallas kernels, on_device(): pl.pallas_call(pack_kernel, out_shape=[shape(8, EDGE, C)] * 2, in_specs=[...  1.95 us
  transfers between devices with their start and end apart: 5, of which 4 were waited for; matrix products, arithmetic and copies ran while one was open for 0% of the time, Pallas kernels for 0%

commit v1 on v0

v1 whole, which is shorter than its diff:
```python
import jax
import jax.numpy as jnp
from jax import lax
from jax.experimental import pallas as pl
from jax.experimental.pallas import tpu as pltpu
from jax.sharding import PartitionSpec as P

EPSILON = 1e-06
C = 384
FRAMES = 4
COLS = 12
ROWS = 8
MAIN = COLS * ROWS
EDGE = COLS * 2
TAPS = 9
K = TAPS * C
TILE = 256
STEPS = -(-K // TILE)
BF16 = jnp.bfloat16
F32 = jnp.float32
VMEM = pl.BlockSpec(memory_space=pltpu.VMEM)
HBM = pl.BlockSpec(memory_space=pltpu.HBM)


def rolled(value, shift, axis):
    shift = shift % value.shape[axis]
    return pltpu.roll(value, shift, axis) if shift else value


def rows_out(main, first):
    split = main.reshape(3, 4, ROWS, C)
    group = lax.broadcasted_iota(jnp.int32, (3, ROWS, C), 1) // 2
    out = None
    for q in range(4):
        piece = rolled(split[:, q], 2 * q - first, 1)
        out = piece if out is None else jnp.where(group == q, piece, out)
    return out.reshape(EDGE, C)


def spread(edge, which, to):
    split = edge.reshape(3, ROWS, C)
    pieces = [rolled(split, to - (2 * q + which), 1) for q in range(4)]
    return jnp.stack(pieces, axis=1).reshape(COLS, ROWS, C)


def shifted_row(main, b, before, before_which, after, after_which):
    if b == 1:
        return main
    split = main.reshape(COLS, ROWS, C)
    place = lax.broadcasted_iota(jnp.int32, (COLS, ROWS, C), 1)
    if b == 0:
        moved = jnp.where(place == 0, spread(before, before_which, 0), rolled(split, 1, 1))
    else:
        moved = jnp.where(place == ROWS - 1, spread(after, after_which, ROWS - 1), rolled(split, -1, 1))
    return moved.reshape(MAIN, C)


def column_taps(main):
    zeros = jnp.zeros((ROWS, C), F32)
    return [
        jnp.concatenate([zeros, main[: MAIN - ROWS]], axis=0),
        main,
        jnp.concatenate([main[ROWS:], zeros], axis=0),
    ]


def edge_column_taps(edge):
    place = lax.broadcasted_iota(jnp.int32, (EDGE, C), 0)
    return [
        jnp.where(place < 2, 0.0, rolled(edge, 2, 0)),
        edge,
        jnp.where(place >= EDGE - 2, 0.0, rolled(edge, -2, 0)),
    ]


def edge_pair(top, bottom):
    even = lax.broadcasted_iota(jnp.int32, (EDGE, C), 0) % 2 == 0
    return jnp.where(even, rolled(top, -1, 0), rolled(bottom, 1, 0))


def normed(values, gain):
    factor = lax.rsqrt(jnp.mean(values * values, axis=-1, keepdims=True) + EPSILON)
    v = values * factor * gain
    return v / (1.0 + jnp.exp(-v))


def push_weights(weights, a, step, slot):
    at = step * TILE
    depth = min(TILE, K - at)
    left = weights[a, at : at + depth, 0:TILE]
    right = weights[a, at : at + depth, TILE:C]
    right = jnp.concatenate([right, right], axis=1)
    if depth < TILE:
        empty = jnp.zeros((TILE - depth, TILE), BF16)
        left = jnp.concatenate([left, empty], axis=0)
        right = jnp.concatenate([right, empty], axis=0)
    pltpu.matmul_push_rhs(left, slot, 0)
    pltpu.matmul_push_rhs(right, slot, 1)


def multiply(accumulators, operand, index, step, slot):
    at = step * TILE
    depth = min(TILE, K - at)
    rows = operand[index][:, at : at + depth] if isinstance(operand, list) else operand[index, :, at : at + depth]
    if depth < TILE:
        rows = jnp.concatenate([rows, rows], axis=1)
    for accumulator in accumulators:
        pltpu.matmul_acc_lhs(accumulator, rows, load_staged_rhs=slot)


def popped(accumulators):
    return jnp.concatenate([pltpu.matmul_pop(accumulators[0]), pltpu.matmul_pop(accumulators[1])[:, : C - TILE]], axis=1)


def woven(steps, thunks):
    order, done = [], 0
    for i, step in enumerate(steps):
        order.append(step)
        due = (i + 1) * len(thunks) // len(steps)
        order += thunks[done:due]
        done = due
    return order


class Section:
    def __init__(self, refs, accumulators, live, at_top, at_bottom):
        self.__dict__.update(refs)
        self.live, self.at_top, self.at_bottom = live, at_top, at_bottom
        frames = FRAMES
        self.sums1 = [(accumulators[f], accumulators[frames + f]) for f in range(frames)]
        self.sums2 = [(accumulators[2 * frames + f], accumulators[3 * frames + f]) for f in range(frames)]
        at = 4 * frames
        self.edges1 = [(accumulators[at + i], accumulators[at + 2 + i]) for i in range(2)]
        self.pending = None
        self.slot = 0

    def norm_first(self, f):
        keep = f < self.live
        gain = self.gain1[...]
        values = jnp.where(keep, self.x[f].astype(F32), 0.0)
        self.window1[f + 2, 0:MAIN] = normed(values, gain).astype(BF16)

    def norm_first_halo(self, f):
        keep = f < self.live
        gain = self.gain1[...]
        top = jnp.where(keep & jnp.logical_not(self.at_top), self.tops[f].astype(F32), 0.0)
        bottom = jnp.where(keep & jnp.logical_not(self.at_bottom), self.bottoms[f].astype(F32), 0.0)
        values = jnp.concatenate([top, bottom], axis=0)
        self.window1[f + 2, MAIN : MAIN + 2 * EDGE] = normed(values, gain).astype(BF16)

    def build_first_edges(self, g):
        main = self.window1[g, 0:MAIN].astype(F32)
        halo = self.window1[g, MAIN : MAIN + 2 * EDGE].astype(F32)
        top, bottom = halo[:EDGE], halo[EDGE:]
        even = lax.broadcasted_iota(jnp.int32, (EDGE, C), 0) % 2 == 0
        self.edge_rows[g, 0] = jnp.where(even, top, rows_out(main, 6))
        self.edge_rows[g, 1] = edge_pair(top, bottom)
        self.edge_rows[g, 2] = jnp.where(even, rows_out(main, 0), bottom)

    def build_first_pair(self, g, b):
        taps = [edge_column_taps(self.edge_rows[g + i, b]) for i in range(2)]
        for c in range(3):
            at = (3 * b + c) * C
            rows = jnp.concatenate([taps[0][c], taps[1][c]], axis=0)
            self.edges[g, :, at : at + C] = rows.astype(BF16)

    def build_first(self, g, b):
        main = self.window1[g, 0:MAIN].astype(F32)
        halo = self.window1[g, MAIN : MAIN + 2 * EDGE].astype(F32)
        self.build(self.operand1, g, b, main, halo[:EDGE], 1, halo[EDGE:], 0)

    def build_second(self, g, b):
        main = self.window2[g].astype(F32)
        edge = self.hidden_edges[g]
        self.build(self.operand2, g, b, main, edge, 0, edge, 1)

    def build(self, operand, g, b, main, before, before_which, after, after_which):
        rows = shifted_row(main, b, before, before_which, after, after_which)
        for c, taps in enumerate(column_taps(rows)):
            at = (3 * b + c) * C
            operand[g, :, at : at + C] = taps.astype(BF16)

    def first_thunks(self, pair, cached=False):
        out = []
        for g in (pair, pair + 1):
            if not cached:
                out += [lambda f=g - 2: self.norm_first(f), lambda f=g - 2: self.norm_first_halo(f)]
        for g in (pair, pair + 1):
            out += [lambda g=g: self.build_first_edges(g)]
            out += [lambda g=g, b=b: self.build_first(g, b) for b in range(3)]
        starts = [pair] if pair == 0 else [pair - 1, pair]
        out += [lambda g=g, b=b: self.build_first_pair(g, b) for g in starts for b in range(3)]
        return out

    def second_thunks(self, pair, cached=False):
        out = []
        if not cached:
            out += [lambda f=f: self.norm_second(f) for f in (pair - 2, pair - 1)]
            out += [lambda i=pair // 2 - 1: self.norm_second_edges(i)]
        out += [lambda g=g, b=b: self.build_second(g, b) for g in (pair, pair + 1) for b in range(3)]
        return out

    def norm_second(self, f):
        hidden = popped(self.sums1[f]) + self.bias1[...]
        if self.early1 is not None and f < 2:
            hidden = hidden + self.early1[f]
        hidden = jnp.where(f < self.live, hidden, 0.0)
        self.window2[f + 2] = normed(hidden, self.gain2[...]).astype(BF16)

    def norm_second_edges(self, i):
        hidden = popped(self.edges1[i]) + self.bias1[...]
        if self.early1 is not None and i == 0:
            hidden = hidden + self.early_edges[...]
        place = lax.broadcasted_iota(jnp.int32, (2 * EDGE, C), 0)
        outside = ((place % 2 == 0) & self.at_top) | ((place % 2 == 1) & self.at_bottom)
        hidden = jnp.where(outside, 0.0, hidden)
        values = normed(hidden, self.gain2[...]).astype(BF16).astype(F32)
        for j in range(2):
            f = 2 * i + j
            self.hidden_edges[f + 2] = jnp.where(f < self.live, values[j * EDGE : (j + 1) * EDGE], 0.0)

    def phase(self, conv, pair):
        weights = (self.weights1, self.weights2)[conv]
        operand = (self.operand1, self.operand2)[conv]
        sums = (self.sums1, self.sums2)[conv]
        steps = []
        for a in range(3):
            work = [(sums[g - a], operand, g) for g in (pair, pair + 1) if 0 <= g - a < FRAMES]
            if conv == 0:
                for i in range(2):
                    if pair <= 2 * i + a + 1 < pair + 2:
                        work.append((self.edges1[i], self.edges, 2 * i + a))
            if work:
                steps += [(conv, a, step, weights, work) for step in range(STEPS)]
        return steps

    def run(self, order):
        steps = [entry for entry in order if isinstance(entry, tuple)]
        ready = set()

        def push(i):
            conv, a, step, weights, _ = steps[i]
            if (conv, a) not in ready:
                ready.add((conv, a))
                self.wait_weights(conv, a)
            push_weights(weights, a, step, i % 2)

        i = 0
        for entry in order:
            if not isinstance(entry, tuple):
                entry()
                continue
            if i == 0:
                push(0)
            if i + 1 < len(steps):
                push(i + 1)
            _, _, step, _, work = entry
            for n, (accumulators, operand, g) in enumerate(work):
                multiply(accumulators, operand, g, step, i % 2 if n == 0 else None)
            i += 1


def pack_kernel(x, first, second, up, down):
    for source, start in ((x, 0), (first, 4), (second, 6)):
        for f in range(source.shape[0]):
            main = source[f].astype(F32)
            up[start + f] = rows_out(main, 0).astype(BF16)
            down[start + f] = rows_out(main, 6).astype(BF16)


SCRATCH = dict(
    window1=pltpu.VMEM((FRAMES + 2, MAIN + 2 * EDGE, C), BF16),
    window2=pltpu.VMEM((FRAMES + 2, MAIN, C), BF16),
    edge_rows=pltpu.VMEM((FRAMES + 2, 3, EDGE, C), F32),
    hidden_edges=pltpu.VMEM((FRAMES + 2, EDGE, C), F32),
    operand1=pltpu.VMEM((FRAMES + 2, MAIN, K), BF16),
    edges=pltpu.VMEM((FRAMES + 1, 2 * EDGE, K), BF16),
    operand2=pltpu.VMEM((FRAMES + 2, MAIN, K), BF16),
    weights1=pltpu.VMEM((3, K, C), BF16),
    weights2=pltpu.VMEM((3, K, C), BF16),
    result=pltpu.VMEM((FRAMES, MAIN, C), BF16),
)
VECTORS = ("bias1", "gain1", "bias2", "gain2")
BLOCKS = dict(x=(FRAMES, MAIN, C), first=(2, MAIN, C), second=(2, MAIN, C), incoming=(FRAMES, MAIN, C))


def tick_kernel(tick, inputs, outputs, scratch, *refs):
    names = list(inputs) + list(outputs) + list(scratch)
    given = dict(zip(names, refs))
    accumulators = given.pop("accumulators", None)
    sems = given["sems"]
    copies = {}
    for name in inputs:
        if name + "_hbm" == name or not name.endswith("_hbm"):
            continue
        inner = name[:-4]
        if inner in ("weights1", "weights2"):
            continue
        copies[inner] = pltpu.make_async_copy(given[name], given[inner], sems.at[len(copies)])
    count = len(copies)
    for conv, inner in enumerate(("weights1", "weights2")):
        for a in range(3):
            copies[conv, a] = pltpu.make_async_copy(
                given[inner + "_hbm"].at[a], given[inner].at[a], sems.at[count + 3 * conv + a]
            )
    for copy in copies.values():
        copy.start()
    segment = lax.axis_index("segment")
    strip = lax.axis_index("strip")
    copies.pop("counts").wait()
    live = given["counts"][7 - segment + tick]
    at_top = strip == 0
    at_bottom = strip == lax.axis_size("strip") - 1

    def body(*accumulators):
        fields = dict(given)
        fields.setdefault("early1", None)
        work = Section(fields, accumulators, live, at_top, at_bottom)
        work.wait_weights = lambda conv, a: copies[conv, a].wait()
        for name in copies:
            if isinstance(name, str):
                copies[name].wait()
        work.window1[0:2, 0:MAIN] = work.first[...]
        work.window2[0:2] = work.second[...]
        if tick == 0:
            none = jnp.zeros((2, EDGE, C), BF16)
            work.window1[0:2, MAIN : MAIN + EDGE] = jnp.where(at_top, none, work.tops[4:6])
            work.window1[0:2, MAIN + EDGE : MAIN + 2 * EDGE] = jnp.where(at_bottom, none, work.bottoms[4:6])
            for g in range(2):
                work.hidden_edges[g] = edge_pair(
                    jnp.where(at_top, 0.0, work.tops[6 + g].astype(F32)),
                    jnp.where(at_bottom, 0.0, work.bottoms[6 + g].astype(F32)),
                )
        else:
            work.window1[0:2, MAIN : MAIN + 2 * EDGE] = work.first_halo[...]
            for g in range(2):
                work.hidden_edges[g] = work.second_edge[g].astype(F32)
        order = work.first_thunks(0, cached=True)
        order += woven(work.phase(0, 0), work.first_thunks(2))
        order += woven(work.phase(0, 2), work.first_thunks(4) + work.second_thunks(0, cached=True))
        order += woven(work.phase(0, 4), work.second_thunks(2))
        order += woven(work.phase(1, 0), work.second_thunks(4))
        order += work.phase(1, 2) + work.phase(1, 4)
        work.run(order)
        bias2 = work.bias2[...]
        for f in range(FRAMES):
            result = popped(work.sums2[f]) + bias2 + work.x[f].astype(F32)
            result = jnp.where(f < live, result, 0.0).astype(BF16)
            work.result[f] = result
            if tick == 0:
                last = segment == lax.axis_size("segment") - 1
                passed = jnp.where(last, work.incoming[f].astype(F32), result.astype(F32))
                work.send[f] = passed.astype(BF16)
                work.send_up[f] = rows_out(passed, 0).astype(BF16)
                work.send_down[f] = rows_out(passed, 6).astype(BF16)

    shapes = [MAIN] * (4 * FRAMES) + [2 * EDGE] * 4
    units = ([0] * FRAMES + [1] * FRAMES) * 2 + [0, 0, 1, 1]
    pl.run_scoped(body, *[pltpu.ACC(unit)((rows, TILE), F32) for unit, rows in zip(units, shapes)])
    copy = pltpu.make_async_copy(given["result"], given["whole"].at[tick], sems.at[0])
    copy.start()
    for i in range(2):
        given["first_next"][i] = given["window1"][live + i, 0:MAIN]
        given["second_next"][i] = given["window2"][live + i]
        if tick == 0:
            given["halo_next"][i] = given["window1"][live + i, MAIN : MAIN + 2 * EDGE]
            given["edge_next"][i] = given["hidden_edges"][live + i].astype(BF16)
    copy.wait()


def shape(*dims):
    return jax.ShapeDtypeStruct(dims, BF16)


def run_tick(tick, operands, out_shapes):
    inputs = list(operands)
    outputs = list(out_shapes)
    scratch = dict(SCRATCH)
    for name in inputs:
        inner = name[:-4]
        if name.endswith("_hbm") and inner in BLOCKS:
            scratch[inner] = pltpu.VMEM(BLOCKS[inner], BF16)
        if name == "counts_hbm":
            scratch["counts"] = pltpu.SMEM((9,), jnp.int32)
        if name.endswith("_hbm") and inner in VECTORS:
            scratch[inner] = pltpu.VMEM((1, C), F32)
    scratch["sems"] = pltpu.SemaphoreType.DMA((16,))
    places = [HBM if n.endswith("_hbm") or n == "base" else VMEM for n in inputs]
    operands = {
        n: pltpu.with_memory_space_constraint(v, pltpu.HBM) if n.endswith("_hbm") else v for n, v in operands.items()
    }
    aliases = {inputs.index("base"): outputs.index("whole")} if "base" in inputs else {}
    return pl.pallas_call(
        lambda *refs: tick_kernel(tick, inputs, outputs, scratch, *refs),
        out_shape=list(out_shapes.values()),
        in_specs=places,
        out_specs=[HBM if n == "whole" else VMEM for n in outputs],
        input_output_aliases=aliases,
        scratch_shapes=list(scratch.values()),
        compiler_params=pltpu.CompilerParams(vmem_limit_bytes=48 << 20),
        name=f"tick{tick}",
    )(*operands.values())


def flat(array):
    frames = array.shape[0]
    return array.transpose(0, 2, 1, 3).reshape(frames, MAIN, C)


def unflat(array):
    frames = array.shape[0]
    return array.reshape(frames, COLS, ROWS, C).transpose(0, 2, 1, 3)


def on_device(
    held_blocks,
    incoming,
    frame_counts,
    first_cache,
    second_cache,
    first_kernel,
    first_bias,
    first_gain,
    second_kernel,
    second_bias,
    second_gain,
):
    segments = lax.axis_size("segment")
    strips = lax.axis_size("strip")
    x = flat(held_blocks[0])
    fresh = flat(incoming[0])
    first = flat(first_cache[0])
    second = flat(second_cache[0])
    params = dict(
        bias1_hbm=first_bias,
        gain1_hbm=first_gain,
        bias2_hbm=second_bias,
        gain2_hbm=second_gain,
        weights1_hbm=first_kernel[0].reshape(3, K, C),
        weights2_hbm=second_kernel[0].reshape(3, K, C),
    )
    up, down = pl.pallas_call(
        pack_kernel, out_shape=[shape(8, EDGE, C)] * 2, in_specs=[VMEM] * 3, out_specs=[VMEM] * 2, name="pack"
    )(x, first, second)
    forward = [(i, (i + 1) % strips) for i in range(strips)]
    backward = [(j, i) for i, j in forward]
    tops = lax.ppermute(down, "strip", forward)
    bottoms = lax.ppermute(up, "strip", backward)
    whole, send, send_up, send_down, first, first_halo, second, second_edge = run_tick(
        0,
        dict(
            counts_hbm=frame_counts,
            tops=tops,
            bottoms=bottoms,
            x_hbm=x,
            first_hbm=first,
            second_hbm=second,
            incoming_hbm=fresh,
            **params,
        ),
        dict(
            whole=shape(2, FRAMES, MAIN, C),
            send=shape(FRAMES, MAIN, C),
            send_up=shape(FRAMES, EDGE, C),
            send_down=shape(FRAMES, EDGE, C),
            first_next=shape(2, MAIN, C),
            halo_next=shape(2, 2 * EDGE, C),
            second_next=shape(2, MAIN, C),
            edge_next=shape(2, EDGE, C),
        ),
    )

    def pairs(step):
        return [
            (s * strips + k, (s + 1) % segments * strips + (k + step) % strips)
            for s in range(segments)
            for k in range(strips)
        ]

    axes = ("segment", "strip")
    tops = lax.ppermute(send_down, axes, pairs(1))
    bottoms = lax.ppermute(send_up, axes, pairs(-1))
    x = lax.ppermute(send, axes, pairs(0))
    whole, first, second = run_tick(
        1,
        dict(
            counts_hbm=frame_counts,
            x=x,
            tops=tops,
            bottoms=bottoms,
            first=first,
            first_halo=first_halo,
            second=second,
            second_edge=second_edge,
            base=whole,
            **params,
        ),
        dict(whole=shape(2, FRAMES, MAIN, C), first_next=shape(2, MAIN, C), second_next=shape(2, MAIN, C)),
    )
    return (
        unflat(whole.reshape(2 * FRAMES, MAIN, C)).reshape(2, 1, FRAMES, ROWS, COLS, C),
        unflat(first)[None],
        unflat(second)[None],
    )


def solution(mesh):
    return jax.shard_map(
        on_device,
        mesh=mesh,
        in_specs=(
            P("segment", None, "strip", None, None),
            P(None, None, "strip", None, None),
            P(),
            P("segment", None, "strip", None, None),
            P("segment", None, "strip", None, None),
            P("segment", None, None, None, None, None),
            P("segment", None),
            P("segment", None),
            P("segment", None, None, None, None, None),
            P("segment", None),
            P("segment", None),
        ),
        out_specs=(
            P(None, "segment", None, "strip", None, None),
            P("segment", None, "strip", None, None),
            P("segment", None, "strip", None, None),
        ),
        check_vma=False,
    )
```

time: 64.4 us -> 55.2 us (0.86)
  the two profiles are of different devices: /device:TPU:24 before, /device:TPU:0 now
where the time goes in v1:
time: 55.2 us; the launch traced here: 55.1 us
  Pallas kernels  31 us (56%)
  starting transfers between devices  12.8 us (23%)
  waiting for transfers between devices  10.4 us (19%)
  between operations  0.82 us (1%)
    pallas_call x2, Pallas kernels, run_tick(): pl.pallas_call(lambda *refs: tick_kernel(tick, inputs, outputs, scratch,...  29.1 us
    ppermute x1, waiting for transfers between devices, on_device(): tops = lax.ppermute(send_down, axes, pairs(1))  6.37 us
    ppermute x1, starting transfers between devices, on_device(): bottoms = lax.ppermute(send_up, axes, pairs(-1))  6.18 us
    ppermute x1, starting transfers between devices, on_device(): bottoms = lax.ppermute(up, 'strip', backward)  4.91 us
    ppermute x1, waiting for transfers between devices, on_device(): tops = lax.ppermute(down, 'strip', forward)  4.05 us
    pallas_call x1, Pallas kernels, on_device(): pl.pallas_call(pack_kernel, out_shape=[shape(8, EDGE, C)] * 2, in_specs=[...  1.95 us
    ppermute x1, starting transfers between devices, on_device(): tops = lax.ppermute(down, 'strip', forward)  1.66 us
  transfers between devices with their start and end apart: 5, of which 2 were waited for; matrix products, arithmetic and copies ran while one was open for 0% of the time, Pallas kernels for 0%

profile of v1, /device:TPU:0, one launch (start us, length us, event | category | flops | bytes accessed | tf_op | source)
XLA Modules:
  0.0 55.1 jit_solution(6980451381352588498)
XLA Ops:
  0.6 1.9 %pack.1 = (bf16[8,24,384]{2,1,0:T(8,128)(2,1)}, bf16[8,24,384]{2,1,0:T(8,128)(2,1)}) custom-call(bf16[4,96,384]{2,1,0:T(8,128)(2,1)} %bitcast.41, bf16[2,96,384]{2,1,0:T(8,128)(2,1)} %bitcast.44, bf16[2,96,384]{2,1,0:T(8,128)(2,1)} %bitcast.46), custom_call_target="tpu_custom_call" | custom-call | tf_op jit(solution)/shard_map/pack/pallas_call | solution.py:442
  2.6 1.7 %collective-permute-start = (bf16[8,24,384]{2,1,0:T(8,128)(2,1)}, bf16[8,24,384]{2,1,0:T(8,128)(2,1)S(1)}, u32[]{:S(2)}, u32[]{:S(2)}) collective-permute-start(bf16[8,24,384]{2,1,0:T(8,128)(2,1)} %get-tuple-element.16), channel_id=1, source_target_pairs={{0,1},{1,2},{2,3},{3,4},{4,5},{5,6},{6,7},{7,8},{8,9},{9,10},{10,1... | collective-permute-start | bytes 442376 | tf_op jit(solution)/shard_map/ppermute | solution.py:447
  4.2 4.9 %collective-permute-start.1 = (bf16[8,24,384]{2,1,0:T(8,128)(2,1)}, bf16[8,24,384]{2,1,0:T(8,128)(2,1)S(1)}, u32[]{:S(2)}, u32[]{:S(2)}) collective-permute-start(bf16[8,24,384]{2,1,0:T(8,128)(2,1)} %get-tuple-element.17), channel_id=1, source_target_pairs={{1,0},{2,1},{3,2},{4,3},{5,4},{6,5},{7,6},{8,7},{9,8},{10,9},{11,1... | collective-permute-start | bytes 442376 | tf_op jit(solution)/shard_map/ppermute | solution.py:448
  9.2 4.1 %collective-permute-done.refs_1_ = bf16[8,24,384]{2,1,0:T(8,128)(2,1)S(1)} collective-permute-done((bf16[8,24,384]{2,1,0:T(8,128)(2,1)}, bf16[8,24,384]{2,1,0:T(8,128)(2,1)S(1)}, u32[]{:S(2)}, u32[]{:S(2)}) %collective-permute-start) | collective-permute-done | bytes 147488 | tf_op jit(solution)/shard_map/ppermute | solution.py:447
  13.2 0.0 collective-permute-done.1.refs_2_
  13.2 14.4 %tick0.1 = (bf16[2,4,96,384]{3,2,1,0:T(8,128)(2,1)}, bf16[4,96,384]{2,1,0:T(8,128)(2,1)S(1)}, bf16[4,24,384]{2,1,0:T(8,128)(2,1)S(1)}, bf16[4,24,384]{2,1,0:T(8,...) custom-call(s32[9]{0:T(128)} %refs_0_.3, ...), custom_call_target="tpu_custom_call" | custom-call | tf_op jit(solution)/shard_map/tick0/pallas_call | solution.py:393
  27.7 0.0 collective-permute-start.2
  27.7 0.1 collective-permute-start.3
  27.8 6.2 %collective-permute-start.4 = (bf16[4,24,384]{2,1,0:T(8,128)(2,1)S(1)}, bf16[4,24,384]{2,1,0:T(8,128)(2,1)S(1)}, u32[]{:S(2)}, u32[]{:S(2)}) collective-permute-start(bf16[4,24,384]{2,1,0:T(8,128)(2,1)S(1)} %get-tuple-element.20), channel_id=1, source_target_pairs={{0,31},{1,16},{2,17},{3,18},{4,19},{5,20},{6,21},{7,22},{8,23},{9,... | collective-permute-start | bytes 221192 | tf_op jit(solution)/shard_map/ppermute | solution.py:482
  33.9 6.4 %collective-permute-done.3.refs_2_ = bf16[4,24,384]{2,1,0:T(8,128)(2,1)S(1)} collective-permute-done((bf16[4,24,384]{2,1,0:T(8,128)(2,1)S(1)}, bf16[4,24,384]{2,1,0:T(8,128)(2,1)S(1)}, u32[]{:S(2)}, u32[]{:S(2)}) %collective-permute-start.3) | collective-permute-done | bytes 73760 | tf_op jit(solution)/shard_map/ppermute | solution.py:481
  40.3 0.0 collective-permute-done.4.refs_3_
  40.3 0.0 collective-permute-done.2.refs_1_
  40.3 14.6 %tick1.1 = (bf16[2,4,96,384]{3,2,1,0:T(8,128)(2,1)}, bf16[2,96,384]{2,1,0:T(8,128)(2,1)}, bf16[2,96,384]{2,1,0:T(8,128)(2,1)}) custom-call(s32[9]{0:T(128)} %refs_0_.3, bf16[4,96,384]{2,1,0:T(8,128)(2,1)S(1)} %collective-permute-done.2.refs_1_, bf16[4,24,384]{2,1,0:T(8,128)(2,1)S(1)} %collective-permute-done.3.refs_2_, ...), custom_call_target="tpu_custom_call", output_to_operand_aliasing={{0}: (8, {})} | custom-call | tf_op jit(solution)/shard_map/tick1/pallas_call | solution.py:393
Async XLA Ops:
  2.6 10.6 %collective-permute-start = (bf16[8,24,384]{2,1,0:T(8,128)(2,1)}, bf16[8,24,384]{2,1,0:T(8,128)(2,1)S(1)}, u32[]{:S(2)}, u32[]{:S(2)}) collective-permute-start(bf16[8,24,384]{2,1,0:T(8,128)(2,1)} %get-tuple-element.16), channel_id=1, source_target_pairs={{0,1},{1,2},{2,3},{3,4},{4,5},{5,6},{6,7},{7,8},{8,9},{9,10},{10,1... | collective-permute-start | bytes 442376 | tf_op jit(solution)/shard_map/ppermute | solution.py:447
  4.2 9.0 %collective-permute-start.1 = (bf16[8,24,384]{2,1,0:T(8,128)(2,1)}, bf16[8,24,384]{2,1,0:T(8,128)(2,1)S(1)}, u32[]{:S(2)}, u32[]{:S(2)}) collective-permute-start(bf16[8,24,384]{2,1,0:T(8,128)(2,1)} %get-tuple-element.17), channel_id=1, source_target_pairs={{1,0},{2,1},{3,2},{4,3},{5,4},{6,5},{7,6},{8,7},{9,8},{10,9},{11,1... | collective-permute-start | bytes 442376 | tf_op jit(solution)/shard_map/ppermute | solution.py:448
  27.7 12.7 %collective-permute-start.2 = (bf16[4,96,384]{2,1,0:T(8,128)(2,1)S(1)}, bf16[4,96,384]{2,1,0:T(8,128)(2,1)S(1)}, u32[]{:S(2)}, u32[]{:S(2)}) collective-permute-start(bf16[4,96,384]{2,1,0:T(8,128)(2,1)S(1)} %get-tuple-element.18), channel_id=1, source_target_pairs={{0,16},{1,17},{2,18},{3,19},{4,20},{5,21},{6,22},{7,23},{8,24},{9,... | collective-permute-start | bytes 884744 | tf_op jit(solution)/shard_map/ppermute | solution.py:483
  27.7 12.6 %collective-permute-start.3 = (bf16[4,24,384]{2,1,0:T(8,128)(2,1)S(1)}, bf16[4,24,384]{2,1,0:T(8,128)(2,1)S(1)}, u32[]{:S(2)}, u32[]{:S(2)}) collective-permute-start(bf16[4,24,384]{2,1,0:T(8,128)(2,1)S(1)} %get-tuple-element.19), channel_id=1, source_target_pairs={{0,17},{1,18},{2,19},{3,20},{4,21},{5,22},{6,23},{7,24},{8,25},{9,... | collective-permute-start | bytes 221192 | tf_op jit(solution)/shard_map/ppermute | solution.py:481
  27.8 12.6 %collective-permute-start.4 = (bf16[4,24,384]{2,1,0:T(8,128)(2,1)S(1)}, bf16[4,24,384]{2,1,0:T(8,128)(2,1)S(1)}, u32[]{:S(2)}, u32[]{:S(2)}) collective-permute-start(bf16[4,24,384]{2,1,0:T(8,128)(2,1)S(1)} %get-tuple-element.20), channel_id=1, source_target_pairs={{0,31},{1,16},{2,17},{3,18},{4,19},{5,20},{6,21},{7,22},{8,23},{9,... | collective-permute-start | bytes 221192 | tf_op jit(solution)/shard_map/ppermute | solution.py:482

commit v2 on v1

--- a/solution.py
+++ b/solution.py
@@ -123,16 +123,20 @@
 
 
 class Section:
-    def __init__(self, refs, accumulators, live, at_top, at_bottom):
+    def __init__(self, refs, accumulators, live, even, at_top, at_bottom):
         self.__dict__.update(refs)
-        self.live, self.at_top, self.at_bottom = live, at_top, at_bottom
+        self.live, self.even, self.at_top, self.at_bottom = live, even, at_top, at_bottom
         frames = FRAMES
         self.sums1 = [(accumulators[f], accumulators[frames + f]) for f in range(frames)]
         self.sums2 = [(accumulators[2 * frames + f], accumulators[3 * frames + f]) for f in range(frames)]
         at = 4 * frames
         self.edges1 = [(accumulators[at + i], accumulators[at + 2 + i]) for i in range(2)]
-        self.pending = None
-        self.slot = 0
+
+    def halo(self, f):
+        near, far = self.near[f].astype(F32), self.far[f].astype(F32)
+        top = jnp.where(self.at_top, 0.0, jnp.where(self.even, far, near))
+        bottom = jnp.where(self.at_bottom, 0.0, jnp.where(self.even, near, far))
+        return top, bottom
 
     def norm_first(self, f):
         keep = f < self.live
@@ -143,8 +147,7 @@
     def norm_first_halo(self, f):
         keep = f < self.live
         gain = self.gain1[...]
-        top = jnp.where(keep & jnp.logical_not(self.at_top), self.tops[f].astype(F32), 0.0)
-        bottom = jnp.where(keep & jnp.logical_not(self.at_bottom), self.bottoms[f].astype(F32), 0.0)
+        top, bottom = (jnp.where(keep, rows, 0.0) for rows in self.halo(f))
         values = jnp.concatenate([top, bottom], axis=0)
         self.window1[f + 2, MAIN : MAIN + 2 * EDGE] = normed(values, gain).astype(BF16)
 
@@ -236,13 +239,9 @@
 
     def run(self, order):
         steps = [entry for entry in order if isinstance(entry, tuple)]
-        ready = set()
 
         def push(i):
-            conv, a, step, weights, _ = steps[i]
-            if (conv, a) not in ready:
-                ready.add((conv, a))
-                self.wait_weights(conv, a)
+            _, a, step, weights, _ = steps[i]
             push_weights(weights, a, step, i % 2)
 
         i = 0
@@ -260,12 +259,29 @@
             i += 1
 
 
-def pack_kernel(x, first, second, up, down):
+def load_kernel(first, second, first_out, second_out, sems):
+    copies = [
+        pltpu.make_async_copy(source.at[a], target.at[a], sems.at[i, a])
+        for i, (source, target) in enumerate(((first, first_out), (second, second_out)))
+        for a in range(3)
+    ]
+    for copy in copies:
+        copy.start()
+    for copy in copies:
+        copy.wait()
+
+
+def edges_out(main, even, near, far, f):
+    upper, lower = rows_out(main, 0), rows_out(main, 6)
+    near[f] = jnp.where(even, lower, upper).astype(BF16)
+    far[f] = jnp.where(even, upper, lower).astype(BF16)
+
+
+def pack_kernel(x, first, second, near, far):
+    even = lax.axis_index("strip") % 2 == 0
     for source, start in ((x, 0), (first, 4), (second, 6)):
         for f in range(source.shape[0]):
-            main = source[f].astype(F32)
-            up[start + f] = rows_out(main, 0).astype(BF16)
-            down[start + f] = rows_out(main, 6).astype(BF16)
+            edges_out(source[f].astype(F32), even, near, far, start + f)
 
 
 SCRATCH = dict(
@@ -276,8 +292,6 @@
     operand1=pltpu.VMEM((FRAMES + 2, MAIN, K), BF16),
     edges=pltpu.VMEM((FRAMES + 1, 2 * EDGE, K), BF16),
     operand2=pltpu.VMEM((FRAMES + 2, MAIN, K), BF16),
-    weights1=pltpu.VMEM((3, K, C), BF16),
-    weights2=pltpu.VMEM((3, K, C), BF16),
     result=pltpu.VMEM((FRAMES, MAIN, C), BF16),
 )
 VECTORS = ("bias1", "gain1", "bias2", "gain2")
@@ -294,15 +308,7 @@
         if name + "_hbm" == name or not name.endswith("_hbm"):
             continue
         inner = name[:-4]
-        if inner in ("weights1", "weights2"):
-            continue
         copies[inner] = pltpu.make_async_copy(given[name], given[inner], sems.at[len(copies)])
-    count = len(copies)
-    for conv, inner in enumerate(("weights1", "weights2")):
-        for a in range(3):
-            copies[conv, a] = pltpu.make_async_copy(
-                given[inner + "_hbm"].at[a], given[inner].at[a], sems.at[count + 3 * conv + a]
-            )
     for copy in copies.values():
         copy.start()
     segment = lax.axis_index("segment")
@@ -315,22 +321,16 @@
     def body(*accumulators):
         fields = dict(given)
         fields.setdefault("early1", None)
-        work = Section(fields, accumulators, live, at_top, at_bottom)
-        work.wait_weights = lambda conv, a: copies[conv, a].wait()
-        for name in copies:
-            if isinstance(name, str):
-                copies[name].wait()
+        work = Section(fields, accumulators, live, strip % 2 == 0, at_top, at_bottom)
+        for copy in copies.values():
+            copy.wait()
         work.window1[0:2, 0:MAIN] = work.first[...]
         work.window2[0:2] = work.second[...]
         if tick == 0:
-            none = jnp.zeros((2, EDGE, C), BF16)
-            work.window1[0:2, MAIN : MAIN + EDGE] = jnp.where(at_top, none, work.tops[4:6])
-            work.window1[0:2, MAIN + EDGE : MAIN + 2 * EDGE] = jnp.where(at_bottom, none, work.bottoms[4:6])
             for g in range(2):
-                work.hidden_edges[g] = edge_pair(
-                    jnp.where(at_top, 0.0, work.tops[6 + g].astype(F32)),
-                    jnp.where(at_bottom, 0.0, work.bottoms[6 + g].astype(F32)),
-                )
+                rows = jnp.concatenate(work.halo(4 + g), axis=0)
+                work.window1[g, MAIN : MAIN + 2 * EDGE] = rows.astype(BF16)
+                work.hidden_edges[g] = edge_pair(*work.halo(6 + g))
         else:
             work.window1[0:2, MAIN : MAIN + 2 * EDGE] = work.first_halo[...]
             for g in range(2):
@@ -351,8 +351,7 @@
                 last = segment == lax.axis_size("segment") - 1
                 passed = jnp.where(last, work.incoming[f].astype(F32), result.astype(F32))
                 work.send[f] = passed.astype(BF16)
-                work.send_up[f] = rows_out(passed, 0).astype(BF16)
-                work.send_down[f] = rows_out(passed, 6).astype(BF16)
+                edges_out(passed, work.even, work.send_near, work.send_far, f)
 
     shapes = [MAIN] * (4 * FRAMES) + [2 * EDGE] * 4
     units = ([0] * FRAMES + [1] * FRAMES) * 2 + [0, 0, 1, 1]
@@ -397,7 +396,7 @@
         out_specs=[HBM if n == "whole" else VMEM for n in outputs],
         input_output_aliases=aliases,
         scratch_shapes=list(scratch.values()),
-        compiler_params=pltpu.CompilerParams(vmem_limit_bytes=48 << 20),
+        compiler_params=pltpu.CompilerParams(vmem_limit_bytes=24 << 20),
         name=f"tick{tick}",
     )(*operands.values())
 
@@ -431,27 +430,43 @@
     fresh = flat(incoming[0])
     first = flat(first_cache[0])
     second = flat(second_cache[0])
+    weights1, weights2 = pl.pallas_call(
+        load_kernel,
+        out_shape=[pltpu.VMEM((3, K, C), BF16)] * 2,
+        in_specs=[HBM] * 2,
+        out_specs=[VMEM] * 2,
+        scratch_shapes=[pltpu.SemaphoreType.DMA((2, 3))],
+        compiler_params=pltpu.CompilerParams(vmem_limit_bytes=1 << 20),
+        cost_estimate=pl.CostEstimate(flops=0, bytes_accessed=4 * 3 * K * C, transcendentals=0),
+        name="load",
+    )(
+        *(
+            pltpu.with_memory_space_constraint(kernel[0].reshape(3, K, C), pltpu.HBM)
+            for kernel in (first_kernel, second_kernel)
+        )
+    )
     params = dict(
         bias1_hbm=first_bias,
         gain1_hbm=first_gain,
         bias2_hbm=second_bias,
         gain2_hbm=second_gain,
-        weights1_hbm=first_kernel[0].reshape(3, K, C),
-        weights2_hbm=second_kernel[0].reshape(3, K, C),
+        weights1=weights1,
+        weights2=weights2,
     )
-    up, down = pl.pallas_call(
+    near, far = pl.pallas_call(
         pack_kernel, out_shape=[shape(8, EDGE, C)] * 2, in_specs=[VMEM] * 3, out_specs=[VMEM] * 2, name="pack"
     )(x, first, second)
-    forward = [(i, (i + 1) % strips) for i in range(strips)]
-    backward = [(j, i) for i, j in forward]
-    tops = lax.ppermute(down, "strip", forward)
-    bottoms = lax.ppermute(up, "strip", backward)
-    whole, send, send_up, send_down, first, first_halo, second, second_edge = run_tick(
+    swaps = [
+        [(i, i ^ 1) for i in range(strips)],
+        [(i, (((i + 1) ^ 1) - 1) % strips) for i in range(strips)],
+    ]
+    near, far = (lax.ppermute(rows, "strip", swap) for rows, swap in zip((near, far), swaps))
+    whole, send, send_near, send_far, first, first_halo, second, second_edge = run_tick(
         0,
         dict(
             counts_hbm=frame_counts,
-            tops=tops,
-            bottoms=bottoms,
+            near=near,
+            far=far,
             x_hbm=x,
             first_hbm=first,
             second_hbm=second,
@@ -461,8 +476,8 @@
         dict(
             whole=shape(2, FRAMES, MAIN, C),
             send=shape(FRAMES, MAIN, C),
-            send_up=shape(FRAMES, EDGE, C),
-            send_down=shape(FRAMES, EDGE, C),
+            send_near=shape(FRAMES, EDGE, C),
+            send_far=shape(FRAMES, EDGE, C),
             first_next=shape(2, MAIN, C),
             halo_next=shape(2, 2 * EDGE, C),
             second_next=shape(2, MAIN, C),
@@ -470,24 +485,19 @@
         ),
     )
 
-    def pairs(step):
-        return [
-            (s * strips + k, (s + 1) % segments * strips + (k + step) % strips)
-            for s in range(segments)
-            for k in range(strips)
-        ]
-
-    axes = ("segment", "strip")
-    tops = lax.ppermute(send_down, axes, pairs(1))
-    bottoms = lax.ppermute(send_up, axes, pairs(-1))
-    x = lax.ppermute(send, axes, pairs(0))
+    def onward(rows, swap):
+        pairs = [(s * strips + i, (s + 1) % segments * strips + j) for s in range(segments) for i, j in swap]
+        return lax.ppermute(rows, ("segment", "strip"), pairs)
+
+    x = onward(send, [(i, i) for i in range(strips)])
+    near, far = (onward(rows, swap) for rows, swap in zip((send_near, send_far), swaps))
     whole, first, second = run_tick(
         1,
         dict(
             counts_hbm=frame_counts,
             x=x,
-            tops=tops,
-            bottoms=bottoms,
+            near=near,
+            far=far,
             first=first,
             first_halo=first_halo,
             second=second,

time: 55.2 us -> 53.9 us (0.976)
  waiting for transfers between devices: 10.4 us -> 7.17 us
  Pallas kernels: 31 us -> 34.1 us
  starting transfers between devices: 12.8 us -> 11.7 us
    pallas_call x0 -> x1, Pallas kernels: none -> 5.66 us  [on_device(): pl.pallas_call(load_kernel, out_shape=[pltpu.VMEM((3, K, C), BF16)] * 2,...]
    ppermute x5, waiting for transfers between devices: 10.4 us -> 7.17 us  [the longest x3 7.16 us: onward(): return lax.ppermute(rows, ('segment', 'strip'), pairs)]
    pallas_call x2, Pallas kernels: 29.1 us -> 26.5 us  [run_tick(): pl.pallas_call(lambda *refs: tick_kernel(tick, inputs, outputs, scratch,...]
    ppermute x5, starting transfers between devices: 12.8 us -> 11.7 us  [the longest x2 7.31 us: on_device(): lax.ppermute(rows, 'strip', swap)]
  transfers between devices with their start and end apart: 5 -> 5, of which waited for: 2 -> 2; matrix products, arithmetic and copies ran while one was open for 0% -> 0% of each run, Pallas kernels for 0% -> 11%
where the time goes in v2:
time: 53.9 us; the launch traced here: 53.8 us
  Pallas kernels  34.1 us (63%)
  starting transfers between devices  11.7 us (22%)
  waiting for transfers between devices  7.17 us (13%)
  between operations  0.84 us (2%)
    pallas_call x2, Pallas kernels, run_tick(): pl.pallas_call(lambda *refs: tick_kernel(tick, inputs, outputs, scratch,...  26.5 us
    ppermute x2, starting transfers between devices, on_device(): lax.ppermute(rows, 'strip', swap)  7.31 us
    ppermute x3, waiting for transfers between devices, onward(): return lax.ppermute(rows, ('segment', 'strip'), pairs)  7.16 us
    pallas_call x1, Pallas kernels, on_device(): pl.pallas_call(load_kernel, out_shape=[pltpu.VMEM((3, K, C), BF16)] * 2,...  5.66 us
    ppermute x3, starting transfers between devices, onward(): return lax.ppermute(rows, ('segment', 'strip'), pairs)  4.34 us
    pallas_call x1, Pallas kernels, on_device(): pl.pallas_call(pack_kernel, out_shape=[shape(8, EDGE, C)] * 2, in_specs=[...  1.97 us
  transfers between devices with their start and end apart: 5, of which 2 were waited for; matrix products, arithmetic and copies ran while one was open for 0% of the time, Pallas kernels for 11%

profile of v2, /device:TPU:0, one launch (start us, length us, event | category | flops | bytes accessed | tf_op | source)
XLA Modules:
  0.0 53.8 jit_solution(5459012001261638847)
XLA Ops:
  0.6 2.0 %pack.1 = (bf16[8,24,384]{2,1,0:T(8,128)(2,1)}, bf16[8,24,384]{2,1,0:T(8,128)(2,1)}) custom-call(bf16[4,96,384]{2,1,0:T(8,128)(2,1)} %bitcast.39, bf16[2,96,384]{2,1,0:T(8,128)(2,1)} %bitcast.42, bf16[2,96,384]{2,1,0:T(8,128)(2,1)} %bitcast.44), custom_call_target="tpu_custom_call" | custom-call | tf_op jit(solution)/shard_map/pack/pallas_call | solution.py:456
  2.6 1.7 %collective-permute-start = (bf16[8,24,384]{2,1,0:T(8,128)(2,1)}, bf16[8,24,384]{2,1,0:T(8,128)(2,1)S(1)}, u32[]{:S(2)}, u32[]{:S(2)}) collective-permute-start(bf16[8,24,384]{2,1,0:T(8,128)(2,1)} %get-tuple-element.18), channel_id=1, source_target_pairs={{0,1},{1,0},{2,3},{3,2},{4,5},{5,4},{6,7},{7,6},{8,9},{9,8},{10,11... | collective-permute-start | bytes 442376 | tf_op jit(solution)/shard_map/ppermute | solution.py:463
  4.3 5.7 %collective-permute-start.1 = (bf16[8,24,384]{2,1,0:T(8,128)(2,1)}, bf16[8,24,384]{2,1,0:T(8,128)(2,1)S(1)}, u32[]{:S(2)}, u32[]{:S(2)}) collective-permute-start(bf16[8,24,384]{2,1,0:T(8,128)(2,1)} %get-tuple-element.19), channel_id=1, source_target_pairs={{0,15},{1,2},{2,1},{3,4},{4,3},{5,6},{6,5},{7,8},{8,7},{9,10},{10,... | collective-permute-start | bytes 442376 | tf_op jit(solution)/shard_map/ppermute | solution.py:463
  9.9 5.7 %load.1 = (bf16[3,3456,384]{2,1,0:T(8,128)(2,1)S(1)}, bf16[3,3456,384]{2,1,0:T(8,128)(2,1)S(1)}) custom-call(bf16[3,3456,384]{2,1,0:T(8,128)(2,1)} %bitcast.37, bf16[3,3456,384]{2,1,0:T(8,128)(2,1)} %bitcast.38), custom_call_target="tpu_custom_call" | custom-call | bytes 15925248 | tf_op jit(solution)/shard_map/load/pallas_call | solution.py:433
  15.6 0.0 collective-permute-done.refs_1_
  15.6 0.0 collective-permute-done.1.refs_2_
  15.6 13.2 %tick0.1 = (bf16[2,4,96,384]{3,2,1,0:T(8,128)(2,1)}, bf16[4,96,384]{2,1,0:T(8,128)(2,1)S(1)}, bf16[4,24,384]{2,1,0:T(8,128)(2,1)S(1)}, bf16[4,24,384]{2,1,0:T(8,...) custom-call(s32[9]{0:T(128)} %refs_0_.3, ...), custom_call_target="tpu_custom_call" | custom-call | tf_op jit(solution)/shard_map/tick0/pallas_call | solution.py:392
  28.8 0.0 collective-permute-start.2
  28.8 0.1 collective-permute-start.3
  28.9 4.3 %collective-permute-start.4 = (bf16[4,24,384]{2,1,0:T(8,128)(2,1)S(1)}, bf16[4,24,384]{2,1,0:T(8,128)(2,1)S(1)}, u32[]{:S(2)}, u32[]{:S(2)}) collective-permute-start(bf16[4,24,384]{2,1,0:T(8,128)(2,1)S(1)} %get-tuple-element.24), channel_id=1, source_target_pairs={{0,31},{1,18},{2,17},{3,20},{4,19},{5,22},{6,21},{7,24},{8,23},{9,... | collective-permute-start | bytes 221192 | tf_op jit(solution)/shard_map/ppermute | solution.py:490
  33.1 1.7 %collective-permute-done.3.refs_2_ = bf16[4,24,384]{2,1,0:T(8,128)(2,1)S(1)} collective-permute-done((bf16[4,24,384]{2,1,0:T(8,128)(2,1)S(1)}, bf16[4,24,384]{2,1,0:T(8,128)(2,1)S(1)}, u32[]{:S(2)}, u32[]{:S(2)}) %collective-permute-start.3) | collective-permute-done | bytes 73760 | tf_op jit(solution)/shard_map/ppermute | solution.py:490
  34.9 5.4 %collective-permute-done.4.refs_3_ = bf16[4,24,384]{2,1,0:T(8,128)(2,1)S(1)} collective-permute-done((bf16[4,24,384]{2,1,0:T(8,128)(2,1)S(1)}, bf16[4,24,384]{2,1,0:T(8,128)(2,1)S(1)}, u32[]{:S(2)}, u32[]{:S(2)}) %collective-permute-start.4) | collective-permute-done | bytes 73760 | tf_op jit(solution)/shard_map/ppermute | solution.py:490
  40.3 0.0 collective-permute-done.2.refs_1_
  40.3 13.3 %tick1.1 = (bf16[2,4,96,384]{3,2,1,0:T(8,128)(2,1)}, bf16[2,96,384]{2,1,0:T(8,128)(2,1)}, bf16[2,96,384]{2,1,0:T(8,128)(2,1)}) custom-call(s32[9]{0:T(128)} %refs_0_.3, bf16[4,96,384]{2,1,0:T(8,128)(2,1)S(1)} %collective-permute-done.2.refs_1_, bf16[4,24,384]{2,1,0:T(8,128)(2,1)S(1)} %collective-permute-done.3.refs_2_, ...), custom_call_target="tpu_custom_call", output_to_operand_aliasing={{0}: (8, {})} | custom-call | tf_op jit(solution)/shard_map/tick1/pallas_call | solution.py:392
Async XLA Ops:
  2.6 13.0 %collective-permute-start = (bf16[8,24,384]{2,1,0:T(8,128)(2,1)}, bf16[8,24,384]{2,1,0:T(8,128)(2,1)S(1)}, u32[]{:S(2)}, u32[]{:S(2)}) collective-permute-start(bf16[8,24,384]{2,1,0:T(8,128)(2,1)} %get-tuple-element.18), channel_id=1, source_target_pairs={{0,1},{1,0},{2,3},{3,2},{4,5},{5,4},{6,7},{7,6},{8,9},{9,8},{10,11... | collective-permute-start | bytes 442376 | tf_op jit(solution)/shard_map/ppermute | solution.py:463
  4.3 11.3 %collective-permute-start.1 = (bf16[8,24,384]{2,1,0:T(8,128)(2,1)}, bf16[8,24,384]{2,1,0:T(8,128)(2,1)S(1)}, u32[]{:S(2)}, u32[]{:S(2)}) collective-permute-start(bf16[8,24,384]{2,1,0:T(8,128)(2,1)} %get-tuple-element.19), channel_id=1, source_target_pairs={{0,15},{1,2},{2,1},{3,4},{4,3},{5,6},{6,5},{7,8},{8,7},{9,10},{10,... | collective-permute-start | bytes 442376 | tf_op jit(solution)/shard_map/ppermute | solution.py:463
  28.8 11.5 %collective-permute-start.2 = (bf16[4,96,384]{2,1,0:T(8,128)(2,1)S(1)}, bf16[4,96,384]{2,1,0:T(8,128)(2,1)S(1)}, u32[]{:S(2)}, u32[]{:S(2)}) collective-permute-start(bf16[4,96,384]{2,1,0:T(8,128)(2,1)S(1)} %get-tuple-element.22), channel_id=1, source_target_pairs={{0,16},{1,17},{2,18},{3,19},{4,20},{5,21},{6,22},{7,23},{8,24},{9,... | collective-permute-start | bytes 884744 | tf_op jit(solution)/shard_map/ppermute | solution.py:490
  28.8 6.1 %collective-permute-start.3 = (bf16[4,24,384]{2,1,0:T(8,128)(2,1)S(1)}, bf16[4,24,384]{2,1,0:T(8,128)(2,1)S(1)}, u32[]{:S(2)}, u32[]{:S(2)}) collective-permute-start(bf16[4,24,384]{2,1,0:T(8,128)(2,1)S(1)} %get-tuple-element.23), channel_id=1, source_target_pairs={{0,17},{1,16},{2,19},{3,18},{4,21},{5,20},{6,23},{7,22},{8,25},{9,... | collective-permute-start | bytes 221192 | tf_op jit(solution)/shard_map/ppermute | solution.py:490
  28.9 11.4 %collective-permute-start.4 = (bf16[4,24,384]{2,1,0:T(8,128)(2,1)S(1)}, bf16[4,24,384]{2,1,0:T(8,128)(2,1)S(1)}, u32[]{:S(2)}, u32[]{:S(2)}) collective-permute-start(bf16[4,24,384]{2,1,0:T(8,128)(2,1)S(1)} %get-tuple-element.24), channel_id=1, source_target_pairs={{0,31},{1,18},{2,17},{3,20},{4,19},{5,22},{6,21},{7,24},{8,23},{9,... | collective-permute-start | bytes 221192 | tf_op jit(solution)/shard_map/ppermute | solution.py:490

commit v3 on v2

--- a/solution.py
+++ b/solution.py
@@ -122,6 +122,10 @@
     return order
 
 
+def first_normed(frame, keep, gain):
+    return normed(jnp.where(keep, frame.astype(F32), 0.0), gain).astype(BF16)
+
+
 class Section:
     def __init__(self, refs, accumulators, live, even, at_top, at_bottom):
         self.__dict__.update(refs)
@@ -139,21 +143,18 @@
         return top, bottom
 
     def norm_first(self, f):
-        keep = f < self.live
-        gain = self.gain1[...]
-        values = jnp.where(keep, self.x[f].astype(F32), 0.0)
-        self.window1[f + 2, 0:MAIN] = normed(values, gain).astype(BF16)
+        self.window1[f + 2] = first_normed(self.x[f], f < self.live, self.gain1[...])
 
     def norm_first_halo(self, f):
         keep = f < self.live
         gain = self.gain1[...]
         top, bottom = (jnp.where(keep, rows, 0.0) for rows in self.halo(f))
         values = jnp.concatenate([top, bottom], axis=0)
-        self.window1[f + 2, MAIN : MAIN + 2 * EDGE] = normed(values, gain).astype(BF16)
+        self.halos[f + 2] = normed(values, gain).astype(BF16)
 
     def build_first_edges(self, g):
-        main = self.window1[g, 0:MAIN].astype(F32)
-        halo = self.window1[g, MAIN : MAIN + 2 * EDGE].astype(F32)
+        main = self.window1[g].astype(F32)
+        halo = self.halos[g].astype(F32)
         top, bottom = halo[:EDGE], halo[EDGE:]
         even = lax.broadcasted_iota(jnp.int32, (EDGE, C), 0) % 2 == 0
         self.edge_rows[g, 0] = jnp.where(even, top, rows_out(main, 6))
@@ -168,8 +169,8 @@
             self.edges[g, :, at : at + C] = rows.astype(BF16)
 
     def build_first(self, g, b):
-        main = self.window1[g, 0:MAIN].astype(F32)
-        halo = self.window1[g, MAIN : MAIN + 2 * EDGE].astype(F32)
+        main = self.window1[g].astype(F32)
+        halo = self.halos[g].astype(F32)
         self.build(self.operand1, g, b, main, halo[:EDGE], 1, halo[EDGE:], 0)
 
     def build_second(self, g, b):
@@ -187,7 +188,8 @@
         out = []
         for g in (pair, pair + 1):
             if not cached:
-                out += [lambda f=g - 2: self.norm_first(f), lambda f=g - 2: self.norm_first_halo(f)]
+                out += [lambda f=g - 2: self.norm_first(f)] if self.norms else []
+                out += [lambda f=g - 2: self.norm_first_halo(f)]
         for g in (pair, pair + 1):
             out += [lambda g=g: self.build_first_edges(g)]
             out += [lambda g=g, b=b: self.build_first(g, b) for b in range(3)]
@@ -221,6 +223,12 @@
         for j in range(2):
             f = 2 * i + j
             self.hidden_edges[f + 2] = jnp.where(f < self.live, values[j * EDGE : (j + 1) * EDGE], 0.0)
+
+    def final(self, f):
+        result = popped(self.sums2[f]) + self.bias2[...] + self.x[f].astype(F32)
+        if self.early1 is not None and f < 2:
+            result = result + self.early2[f]
+        return jnp.where(f < self.live, result, 0.0).astype(BF16)
 
     def phase(self, conv, pair):
         weights = (self.weights1, self.weights2)[conv]
@@ -259,18 +267,6 @@
             i += 1
 
 
-def load_kernel(first, second, first_out, second_out, sems):
-    copies = [
-        pltpu.make_async_copy(source.at[a], target.at[a], sems.at[i, a])
-        for i, (source, target) in enumerate(((first, first_out), (second, second_out)))
-        for a in range(3)
-    ]
-    for copy in copies:
-        copy.start()
-    for copy in copies:
-        copy.wait()
-
-
 def edges_out(main, even, near, far, f):
     upper, lower = rows_out(main, 0), rows_out(main, 6)
     near[f] = jnp.where(even, lower, upper).astype(BF16)
@@ -284,121 +280,173 @@
             edges_out(source[f].astype(F32), even, near, far, start + f)
 
 
-SCRATCH = dict(
-    window1=pltpu.VMEM((FRAMES + 2, MAIN + 2 * EDGE, C), BF16),
-    window2=pltpu.VMEM((FRAMES + 2, MAIN, C), BF16),
+WINDOW = (FRAMES + 2, MAIN, C)
+OPERANDS = dict(
     edge_rows=pltpu.VMEM((FRAMES + 2, 3, EDGE, C), F32),
-    hidden_edges=pltpu.VMEM((FRAMES + 2, EDGE, C), F32),
     operand1=pltpu.VMEM((FRAMES + 2, MAIN, K), BF16),
     edges=pltpu.VMEM((FRAMES + 1, 2 * EDGE, K), BF16),
     operand2=pltpu.VMEM((FRAMES + 2, MAIN, K), BF16),
-    result=pltpu.VMEM((FRAMES, MAIN, C), BF16),
 )
 VECTORS = ("bias1", "gain1", "bias2", "gain2")
-BLOCKS = dict(x=(FRAMES, MAIN, C), first=(2, MAIN, C), second=(2, MAIN, C), incoming=(FRAMES, MAIN, C))
-
-
-def tick_kernel(tick, inputs, outputs, scratch, *refs):
-    names = list(inputs) + list(outputs) + list(scratch)
-    given = dict(zip(names, refs))
-    accumulators = given.pop("accumulators", None)
-    sems = given["sems"]
-    copies = {}
-    for name in inputs:
-        if name + "_hbm" == name or not name.endswith("_hbm"):
-            continue
-        inner = name[:-4]
-        copies[inner] = pltpu.make_async_copy(given[name], given[inner], sems.at[len(copies)])
-    for copy in copies.values():
+
+
+def live_frames(counts, tick):
+    return counts[7 - lax.axis_index("segment") + tick]
+
+
+def with_section(given, live, body):
+    strip = lax.axis_index("strip")
+    given = {"early1": None, **given}
+
+    def inner(*accumulators):
+        body(Section(given, accumulators, live, strip % 2 == 0, strip == 0, strip == lax.axis_size("strip") - 1))
+
+    shapes = [MAIN] * (4 * FRAMES) + [2 * EDGE] * 4
+    units = ([0] * FRAMES + [1] * FRAMES) * 2 + [0, 0, 1, 1]
+    pl.run_scoped(inner, *[pltpu.ACC(unit)((rows, TILE), F32) for unit, rows in zip(units, shapes)])
+
+
+def prepare_kernel(r):
+    pairs = [(r[n + "_hbm"], r[n]) for n in ("x", "gain1", "bias1", "gain2", "bias2", "second", "incoming")]
+    pairs += [(r["counts_hbm"], r["counts"]), (r["first_hbm"], r["window1"].at[pl.ds(0, 2)])]
+    pairs += [(r["weights1_hbm"].at[a], r["weights1"].at[a]) for a in range(3)]
+    copies = [pltpu.make_async_copy(source, target, r["sems"].at[i]) for i, (source, target) in enumerate(pairs)]
+    for copy in copies:
         copy.start()
-    segment = lax.axis_index("segment")
-    strip = lax.axis_index("strip")
-    copies.pop("counts").wait()
-    live = given["counts"][7 - segment + tick]
-    at_top = strip == 0
-    at_bottom = strip == lax.axis_size("strip") - 1
-
-    def body(*accumulators):
-        fields = dict(given)
-        fields.setdefault("early1", None)
-        work = Section(fields, accumulators, live, strip % 2 == 0, at_top, at_bottom)
-        for copy in copies.values():
+    copies[7].wait()
+    copies[0].wait()
+    copies[1].wait()
+    live = live_frames(r["counts"], 0)
+    gain = r["gain1"][...]
+    for f in range(FRAMES):
+        r["window1"][f + 2] = first_normed(r["x"][f], f < live, gain)
+    for i, copy in enumerate(copies):
+        if i not in (0, 1, 7):
             copy.wait()
-        work.window1[0:2, 0:MAIN] = work.first[...]
+
+
+def tick0_kernel(r):
+    counting = pltpu.make_async_copy(r["counts_hbm"], r["counts"], r["sems"].at[3])
+    counting.start()
+    copies = [pltpu.make_async_copy(r["weights2_hbm"].at[a], r["weights2"].at[a], r["sems"].at[a]) for a in range(3)]
+    for copy in copies:
+        copy.start()
+    counting.wait()
+    live = live_frames(r["counts"], 0)
+
+    def body(work):
+        work.norms = False
         work.window2[0:2] = work.second[...]
-        if tick == 0:
-            for g in range(2):
-                rows = jnp.concatenate(work.halo(4 + g), axis=0)
-                work.window1[g, MAIN : MAIN + 2 * EDGE] = rows.astype(BF16)
-                work.hidden_edges[g] = edge_pair(*work.halo(6 + g))
-        else:
-            work.window1[0:2, MAIN : MAIN + 2 * EDGE] = work.first_halo[...]
-            for g in range(2):
-                work.hidden_edges[g] = work.second_edge[g].astype(F32)
+        for g in range(2):
+            work.halos[g] = jnp.concatenate(work.halo(4 + g), axis=0).astype(BF16)
+            work.hidden_edges[g] = edge_pair(*work.halo(6 + g))
         order = work.first_thunks(0, cached=True)
         order += woven(work.phase(0, 0), work.first_thunks(2))
         order += woven(work.phase(0, 2), work.first_thunks(4) + work.second_thunks(0, cached=True))
         order += woven(work.phase(0, 4), work.second_thunks(2))
+        at = max(i for i, entry in enumerate(order) if isinstance(entry, tuple))
+        order[at:at] = [copy.wait for copy in copies]
         order += woven(work.phase(1, 0), work.second_thunks(4))
         order += work.phase(1, 2) + work.phase(1, 4)
         work.run(order)
-        bias2 = work.bias2[...]
+        last = lax.axis_index("segment") == lax.axis_size("segment") - 1
         for f in range(FRAMES):
-            result = popped(work.sums2[f]) + bias2 + work.x[f].astype(F32)
-            result = jnp.where(f < live, result, 0.0).astype(BF16)
+            result = work.final(f)
             work.result[f] = result
-            if tick == 0:
-                last = segment == lax.axis_size("segment") - 1
-                passed = jnp.where(last, work.incoming[f].astype(F32), result.astype(F32))
-                work.send[f] = passed.astype(BF16)
-                edges_out(passed, work.even, work.send_near, work.send_far, f)
-
-    shapes = [MAIN] * (4 * FRAMES) + [2 * EDGE] * 4
-    units = ([0] * FRAMES + [1] * FRAMES) * 2 + [0, 0, 1, 1]
-    pl.run_scoped(body, *[pltpu.ACC(unit)((rows, TILE), F32) for unit, rows in zip(units, shapes)])
-    copy = pltpu.make_async_copy(given["result"], given["whole"].at[tick], sems.at[0])
-    copy.start()
+            passed = jnp.where(last, work.incoming[f].astype(F32), result.astype(F32))
+            work.send[f] = passed.astype(BF16)
+            edges_out(passed, work.even, work.send_near, work.send_far, f)
+
+    with_section(r, live, body)
+
+
+def between_kernel(r):
+    writing = pltpu.make_async_copy(r["result"], r["whole"].at[0], r["sems"].at[0])
+    writing.start()
+    counting = pltpu.make_async_copy(r["counts_hbm"], r["counts"], r["sems"].at[1])
+    counting.start()
+    counting.wait()
+    live = live_frames(r["counts"], 0)
     for i in range(2):
-        given["first_next"][i] = given["window1"][live + i, 0:MAIN]
-        given["second_next"][i] = given["window2"][live + i]
-        if tick == 0:
-            given["halo_next"][i] = given["window1"][live + i, MAIN : MAIN + 2 * EDGE]
-            given["edge_next"][i] = given["hidden_edges"][live + i].astype(BF16)
-    copy.wait()
+        r["first"][i] = r["window1_old"][live + i]
+        r["first_halo"][i] = r["halos_old"][live + i]
+        r["second"][i] = r["window2_old"][live + i]
+        r["second_edge"][i] = r["edges_old"][live + i]
+
+    def body(work):
+        order = work.first_thunks(0, cached=True)
+        order += woven(work.phase(0, 0), work.second_thunks(0, cached=True))
+        order += work.phase(1, 0)
+        work.run(order)
+        for f in range(2):
+            work.sum1[f] = popped(work.sums1[f])
+            work.sum2[f] = popped(work.sums2[f])
+        work.sum_edges[...] = popped(work.edges1[0])
+
+    given = dict(r, window1=r["first"], halos=r["first_halo"], window2=r["second"], hidden_edges=r["second_edge"])
+    with_section(given, live, body)
+    writing.wait()
+
+
+def tick1_kernel(r):
+    counting = pltpu.make_async_copy(r["counts_hbm"], r["counts"], r["sems"].at[0])
+    counting.start()
+    counting.wait()
+    live = live_frames(r["counts"], 1)
+    copies = []
+
+    def send(source, target):
+        copies.append(pltpu.make_async_copy(source, target, r["sems"].at[len(copies) + 1]))
+        copies[-1].start()
+
+    def body(work):
+        work.norms = True
+        for i in range(2):
+            work.window1[i] = work.first[i]
+            work.halos[i] = work.first_halo[i]
+            work.window2[i] = work.second[i]
+            work.hidden_edges[i] = work.second_edge[i]
+        order = [lambda: work.build_first_edges(1)] + work.first_thunks(2)
+        order += woven(work.phase(0, 2), work.first_thunks(4))
+        order += [lambda: send(work.window1.at[pl.ds(live, 2)], work.first_next)]
+        order += woven(work.phase(0, 4), work.second_thunks(2))
+        order += woven(work.phase(1, 2), work.second_thunks(4))
+        order += [lambda: send(work.window2.at[pl.ds(live, 2)], work.second_next)]
+        order += work.phase(1, 4)
+        work.run(order)
+        for f in range(FRAMES):
+            work.result[f] = work.final(f)
+            send(work.result.at[f], work.whole.at[1, f])
+        for copy in copies:
+            copy.wait()
+
+    with_section(r, live, body)
+
+
+def call(kernel, operands, outputs, scratch, flops=0, moved=0):
+    inputs = list(operands)
+    names = inputs + list(outputs) + list(scratch)
+    in_hbm = [n.endswith("_hbm") or n == "base" for n in inputs]
+    values = [
+        pltpu.with_memory_space_constraint(v, pltpu.HBM) if n.endswith("_hbm") else v for n, v in operands.items()
+    ]
+    aliases = {inputs.index("base"): list(outputs).index("whole")} if "base" in inputs else {}
+    results = pl.pallas_call(
+        lambda *refs: kernel(dict(zip(names, refs))),
+        out_shape=list(outputs.values()),
+        in_specs=[HBM if there else VMEM for there in in_hbm],
+        out_specs=[HBM if n in ("whole", "first_next", "second_next") else VMEM for n in outputs],
+        input_output_aliases=aliases,
+        scratch_shapes=list(scratch.values()),
+        compiler_params=pltpu.CompilerParams(vmem_limit_bytes=22 << 20),
+        cost_estimate=pl.CostEstimate(flops=flops, bytes_accessed=moved, transcendentals=0),
+        name=kernel.__name__.removesuffix("_kernel"),
+    )(*values)
+    return dict(zip(outputs, results))
 
 
 def shape(*dims):
     return jax.ShapeDtypeStruct(dims, BF16)
-
-
-def run_tick(tick, operands, out_shapes):
-    inputs = list(operands)
-    outputs = list(out_shapes)
-    scratch = dict(SCRATCH)
-    for name in inputs:
-        inner = name[:-4]
-        if name.endswith("_hbm") and inner in BLOCKS:
-            scratch[inner] = pltpu.VMEM(BLOCKS[inner], BF16)
-        if name == "counts_hbm":
-            scratch["counts"] = pltpu.SMEM((9,), jnp.int32)
-        if name.endswith("_hbm") and inner in VECTORS:
-            scratch[inner] = pltpu.VMEM((1, C), F32)
-    scratch["sems"] = pltpu.SemaphoreType.DMA((16,))
-    places = [HBM if n.endswith("_hbm") or n == "base" else VMEM for n in inputs]
-    operands = {
-        n: pltpu.with_memory_space_constraint(v, pltpu.HBM) if n.endswith("_hbm") else v for n, v in operands.items()
-    }
-    aliases = {inputs.index("base"): outputs.index("whole")} if "base" in inputs else {}
-    return pl.pallas_call(
-        lambda *refs: tick_kernel(tick, inputs, outputs, scratch, *refs),
-        out_shape=list(out_shapes.values()),
-        in_specs=places,
-        out_specs=[HBM if n == "whole" else VMEM for n in outputs],
-        input_output_aliases=aliases,
-        scratch_shapes=list(scratch.values()),
-        compiler_params=pltpu.CompilerParams(vmem_limit_bytes=24 << 20),
-        name=f"tick{tick}",
-    )(*operands.values())
 
 
 def flat(array):
@@ -426,91 +474,122 @@
 ):
     segments = lax.axis_size("segment")
     strips = lax.axis_size("strip")
+    swaps = [
+        [(i, i ^ 1) for i in range(strips)],
+        [(i, i if i in (0, strips - 1) else ((i + 1) ^ 1) - 1) for i in range(strips)],
+    ]
     x = flat(held_blocks[0])
-    fresh = flat(incoming[0])
     first = flat(first_cache[0])
     second = flat(second_cache[0])
-    weights1, weights2 = pl.pallas_call(
-        load_kernel,
-        out_shape=[pltpu.VMEM((3, K, C), BF16)] * 2,
-        in_specs=[HBM] * 2,
+    near, far = pl.pallas_call(
+        pack_kernel,
+        out_shape=[pltpu.VMEM((8, EDGE, C), BF16)] * 2,
+        in_specs=[VMEM] * 3,
         out_specs=[VMEM] * 2,
-        scratch_shapes=[pltpu.SemaphoreType.DMA((2, 3))],
-        compiler_params=pltpu.CompilerParams(vmem_limit_bytes=1 << 20),
-        cost_estimate=pl.CostEstimate(flops=0, bytes_accessed=4 * 3 * K * C, transcendentals=0),
-        name="load",
-    )(
-        *(
-            pltpu.with_memory_space_constraint(kernel[0].reshape(3, K, C), pltpu.HBM)
-            for kernel in (first_kernel, second_kernel)
-        )
-    )
-    params = dict(
-        bias1_hbm=first_bias,
-        gain1_hbm=first_gain,
-        bias2_hbm=second_bias,
-        gain2_hbm=second_gain,
-        weights1=weights1,
-        weights2=weights2,
-    )
-    near, far = pl.pallas_call(
-        pack_kernel, out_shape=[shape(8, EDGE, C)] * 2, in_specs=[VMEM] * 3, out_specs=[VMEM] * 2, name="pack"
-    )(x, first, second)
-    swaps = [
-        [(i, i ^ 1) for i in range(strips)],
-        [(i, (((i + 1) ^ 1) - 1) % strips) for i in range(strips)],
-    ]
+        compiler_params=pltpu.CompilerParams(vmem_limit_bytes=8 << 20),
+        name="pack",
+    )(*(pltpu.with_memory_space_constraint(rows, pltpu.HBM) for rows in (x, first, second)))
     near, far = (lax.ppermute(rows, "strip", swap) for rows, swap in zip((near, far), swaps))
-    whole, send, send_near, send_far, first, first_halo, second, second_edge = run_tick(
-        0,
+    counts = dict(counts_hbm=frame_counts)
+    count_scratch = dict(counts=pltpu.SMEM((9,), jnp.int32), sems=pltpu.SemaphoreType.DMA((16,)))
+    block = pltpu.VMEM((FRAMES, MAIN, C), BF16)
+    cached = pltpu.VMEM((2, MAIN, C), BF16)
+    weights = pltpu.VMEM((3, K, C), BF16)
+    ready = call(
+        prepare_kernel,
         dict(
-            counts_hbm=frame_counts,
-            near=near,
-            far=far,
             x_hbm=x,
             first_hbm=first,
             second_hbm=second,
-            incoming_hbm=fresh,
-            **params,
+            incoming_hbm=flat(incoming[0]),
+            bias1_hbm=first_bias,
+            gain1_hbm=first_gain,
+            bias2_hbm=second_bias,
+            gain2_hbm=second_gain,
+            weights1_hbm=first_kernel[0].reshape(3, K, C),
+            **counts,
         ),
         dict(
-            whole=shape(2, FRAMES, MAIN, C),
+            x=block,
+            second=cached,
+            incoming=block,
+            window1=pltpu.VMEM(WINDOW, BF16),
+            weights1=weights,
+            **{n: pltpu.VMEM((1, C), F32) for n in VECTORS},
+        ),
+        count_scratch,
+        moved=2 * 3 * K * C,
+    )
+    vectors = {n: ready[n] for n in VECTORS}
+    done = call(
+        tick0_kernel,
+        dict(**counts, near=near, far=far, weights2_hbm=second_kernel[0].reshape(3, K, C), **ready),
+        dict(
+            weights2=weights,
+            halos=pltpu.VMEM((FRAMES + 2, 2 * EDGE, C), BF16),
+            window2=pltpu.VMEM(WINDOW, BF16),
+            hidden_edges=pltpu.VMEM((FRAMES + 2, EDGE, C), F32),
+            result=block,
             send=shape(FRAMES, MAIN, C),
             send_near=shape(FRAMES, EDGE, C),
             send_far=shape(FRAMES, EDGE, C),
-            first_next=shape(2, MAIN, C),
-            halo_next=shape(2, 2 * EDGE, C),
-            second_next=shape(2, MAIN, C),
-            edge_next=shape(2, EDGE, C),
-        ),
+        ),
+        {**OPERANDS, **count_scratch},
     )
 
     def onward(rows, swap):
         pairs = [(s * strips + i, (s + 1) % segments * strips + j) for s in range(segments) for i, j in swap]
         return lax.ppermute(rows, ("segment", "strip"), pairs)
 
-    x = onward(send, [(i, i) for i in range(strips)])
-    near, far = (onward(rows, swap) for rows, swap in zip((send_near, send_far), swaps))
-    whole, first, second = run_tick(
-        1,
+    x = onward(done["send"], [(i, i) for i in range(strips)])
+    near, far = (onward(done[n], swap) for n, swap in zip(("send_near", "send_far"), swaps))
+    both = dict(weights1=ready["weights1"], weights2=done["weights2"])
+    early = call(
+        between_kernel,
         dict(
-            counts_hbm=frame_counts,
-            x=x,
-            near=near,
-            far=far,
-            first=first,
-            first_halo=first_halo,
-            second=second,
-            second_edge=second_edge,
-            base=whole,
-            **params,
-        ),
+            **counts,
+            window1_old=ready["window1"],
+            halos_old=done["halos"],
+            window2_old=done["window2"],
+            edges_old=done["hidden_edges"],
+            result=done["result"],
+            **both,
+        ),
+        dict(
+            whole=shape(2, FRAMES, MAIN, C),
+            first=cached,
+            first_halo=pltpu.VMEM((2, 2 * EDGE, C), BF16),
+            second=cached,
+            second_edge=pltpu.VMEM((2, EDGE, C), F32),
+            sum1=pltpu.VMEM((2, MAIN, C), F32),
+            sum_edges=pltpu.VMEM((2 * EDGE, C), F32),
+            sum2=pltpu.VMEM((2, MAIN, C), F32),
+        ),
+        {**OPERANDS, **count_scratch},
+        flops=2 * 2 * 3 * MAIN * K * C,
+        moved=2 * 3 * K * C,
+    )
+    whole = early.pop("whole")
+    for name, sums in (("early1", "sum1"), ("early_edges", "sum_edges"), ("early2", "sum2")):
+        early[name] = early.pop(sums)
+    out = call(
+        tick1_kernel,
+        dict(**counts, x=x, near=near, far=far, **early, **both, **vectors, base=whole),
         dict(whole=shape(2, FRAMES, MAIN, C), first_next=shape(2, MAIN, C), second_next=shape(2, MAIN, C)),
+        dict(
+            window1=pltpu.VMEM(WINDOW, BF16),
+            halos=pltpu.VMEM((FRAMES + 2, 2 * EDGE, C), BF16),
+            window2=pltpu.VMEM(WINDOW, BF16),
+            hidden_edges=pltpu.VMEM((FRAMES + 2, EDGE, C), F32),
+            result=block,
+            **OPERANDS,
+            **count_scratch,
+        ),
     )
     return (
-        unflat(whole.reshape(2 * FRAMES, MAIN, C)).reshape(2, 1, FRAMES, ROWS, COLS, C),
-        unflat(first)[None],
-        unflat(second)[None],
+        unflat(out["whole"].reshape(2 * FRAMES, MAIN, C)).reshape(2, 1, FRAMES, ROWS, COLS, C),
+        unflat(out["first_next"])[None],
+        unflat(out["second_next"])[None],
     )
 
 

time: 53.9 us -> 44.9 us (0.83)
  the two profiles are of different devices: /device:TPU:0 before, /device:TPU:96 now
where the time goes in v3:
time: 44.9 us; the launch traced here: 44.8 us
  Pallas kernels  30.1 us (67%)
  starting transfers between devices  8.81 us (20%)
  waiting for transfers between devices  4.99 us (11%)
  between operations  0.84 us (2%)
    pallas_call x4, Pallas kernels, call(): pl.pallas_call(lambda *refs: kernel(dict(zip(names, refs))), out_shape=li...  28.9 us
    ppermute x2, starting transfers between devices, on_device(): lax.ppermute(rows, 'strip', swap)  5.57 us
    ppermute x3, waiting for transfers between devices, onward(): return lax.ppermute(rows, ('segment', 'strip'), pairs)  3.48 us
    ppermute x3, starting transfers between devices, onward(): return lax.ppermute(rows, ('segment', 'strip'), pairs)  3.24 us
    ppermute x2, waiting for transfers between devices, on_device(): lax.ppermute(rows, 'strip', swap)  1.51 us
    pallas_call x1, Pallas kernels, on_device(): pl.pallas_call(pack_kernel, out_shape=[pltpu.VMEM((8, EDGE, C), BF16)] *...  1.26 us
  transfers between devices with their start and end apart: 5, of which 2 were waited for; matrix products, arithmetic and copies ran while one was open for 0% of the time, Pallas kernels for 17%

profile of v3, /device:TPU:96, one launch (start us, length us, event | category | flops | bytes accessed | tf_op | source)
XLA Modules:
  0.0 44.8 jit_solution(12105864428352796203)
XLA Ops:
  0.6 1.3 %pack.1 = (bf16[8,24,384]{2,1,0:T(8,128)(2,1)S(1)}, bf16[8,24,384]{2,1,0:T(8,128)(2,1)S(1)}) custom-call(bf16[4,96,384]{2,1,0:T(8,128)(2,1)} %bitcast.39, bf16[2,96,384]{2,1,0:T(8,128)(2,1)} %bitcast.42, bf16[2,96,384]{2,1,0:T(8,128)(2,1)} %bitcast.44), custom_call_target="tpu_custom_call" | custom-call | tf_op jit(solution)/shard_map/pack/pallas_call | solution.py:484
  1.9 1.7 %collective-permute-start = (bf16[8,24,384]{2,1,0:T(8,128)(2,1)S(1)}, bf16[8,24,384]{2,1,0:T(8,128)(2,1)S(1)}, u32[]{:S(2)}, u32[]{:S(2)}) collective-permute-start(bf16[8,24,384]{2,1,0:T(8,128)(2,1)S(1)} %get-tuple-element.33), channel_id=1, source_target_pairs={{0,1},{1,0},{2,3},{3,2},{4,5},{5,4},{6,7},{7,6},{8,9},{9,8},{10,11... | collective-permute-start | bytes 442376 | tf_op jit(solution)/shard_map/ppermute | solution.py:492
  3.5 3.9 %collective-permute-start.1 = (bf16[8,24,384]{2,1,0:T(8,128)(2,1)S(1)}, bf16[8,24,384]{2,1,0:T(8,128)(2,1)S(1)}, u32[]{:S(2)}, u32[]{:S(2)}) collective-permute-start(bf16[8,24,384]{2,1,0:T(8,128)(2,1)S(1)} %get-tuple-element.34), channel_id=1, source_target_pairs={{0,0},{1,2},{2,1},{3,4},{4,3},{5,6},{6,5},{7,8},{8,7},{9,10},{10,9... | collective-permute-start | bytes 442376 | tf_op jit(solution)/shard_map/ppermute | solution.py:492
  7.5 3.9 %prepare.1 = (bf16[4,96,384]{2,1,0:T(8,128)(2,1)S(1)}, bf16[2,96,384]{2,1,0:T(8,128)(2,1)S(1)}, bf16[4,96,384]{2,1,0:T(8,128)(2,1)S(1)}, bf16[6,96,384]{2,1,0:T(...) custom-call(bf16[4,96,384]{2,1,0:T(8,128)(2,1)} %bitcast.40, ...), custom_call_target="tpu_custom_call" | custom-call | bytes 7962624 | tf_op jit(solution)/shard_map/prepare/pallas_call | solution.py:434
  11.3 0.0 collective-permute-done.refs_1_
  11.3 1.5 %collective-permute-done.1.refs_2_ = bf16[8,24,384]{2,1,0:T(8,128)(2,1)S(1)} collective-permute-done((bf16[8,24,384]{2,1,0:T(8,128)(2,1)S(1)}, bf16[8,24,384]{2,1,0:T(8,128)(2,1)S(1)}, u32[]{:S(2)}, u32[]{:S(2)}) %collective-permute-start.1) | collective-permute-done | bytes 147488 | tf_op jit(solution)/shard_map/ppermute | solution.py:492
  12.8 11.6 %tick0.1 = (bf16[3,3456,384]{2,1,0:T(8,128)(2,1)S(1)}, bf16[6,48,384]{2,1,0:T(8,128)(2,1)S(1)}, bf16[6,96,384]{2,1,0:T(8,128)(2,1)S(1)}, f32[6,24,384]{2,1,0:T(8...) custom-call(s32[9]{0:T(128)} %refs_0_.5, ...), custom_call_target="tpu_custom_call" | custom-call | tf_op jit(solution)/shard_map/tick0/pallas_call | solution.py:434
  24.4 0.0 collective-permute-start.2
  24.4 0.6 %collective-permute-start.3 = (bf16[4,24,384]{2,1,0:T(8,128)(2,1)S(1)}, bf16[4,24,384]{2,1,0:T(8,128)(2,1)S(1)}, u32[]{:S(2)}, u32[]{:S(2)}) collective-permute-start(bf16[4,24,384]{2,1,0:T(8,128)(2,1)S(1)} %get-tuple-element.45), channel_id=1, source_target_pairs={{0,17},{1,16},{2,19},{3,18},{4,21},{5,20},{6,23},{7,22},{8,25},{9,... | collective-permute-start | bytes 221192 | tf_op jit(solution)/shard_map/ppermute | solution.py:542
  25.0 2.7 %collective-permute-start.4 = (bf16[4,24,384]{2,1,0:T(8,128)(2,1)S(1)}, bf16[4,24,384]{2,1,0:T(8,128)(2,1)S(1)}, u32[]{:S(2)}, u32[]{:S(2)}) collective-permute-start(bf16[4,24,384]{2,1,0:T(8,128)(2,1)S(1)} %get-tuple-element.46), channel_id=1, source_target_pairs={{0,16},{1,18},{2,17},{3,20},{4,19},{5,22},{6,21},{7,24},{8,23},{9,... | collective-permute-start | bytes 221192 | tf_op jit(solution)/shard_map/ppermute | solution.py:542
  27.7 3.7 %between.1 = (bf16[2,4,96,384]{3,2,1,0:T(8,128)(2,1)}, bf16[2,96,384]{2,1,0:T(8,128)(2,1)S(1)}, bf16[2,48,384]{2,1,0:T(8,128)(2,1)S(1)}, bf16[2,96,384]{2,1,0:T(...) custom-call(s32[9]{0:T(128)} %refs_0_.5, ...), custom_call_target="tpu_custom_call" | custom-call | flops 1528823808 | bytes 7962624 | tf_op jit(solution)/shard_map/between/pallas_call | solution.py:434
  31.3 0.0 collective-permute-done.3.refs_2_
  31.4 3.4 %collective-permute-done.4.refs_3_ = bf16[4,24,384]{2,1,0:T(8,128)(2,1)S(1)} collective-permute-done((bf16[4,24,384]{2,1,0:T(8,128)(2,1)S(1)}, bf16[4,24,384]{2,1,0:T(8,128)(2,1)S(1)}, u32[]{:S(2)}, u32[]{:S(2)}) %collective-permute-start.4) | collective-permute-done | bytes 73760 | tf_op jit(solution)/shard_map/ppermute | solution.py:542
  34.8 0.0 collective-permute-done.2.refs_1_
  34.8 9.8 %tick1.1 = (bf16[2,4,96,384]{3,2,1,0:T(8,128)(2,1)}, bf16[2,96,384]{2,1,0:T(8,128)(2,1)}, bf16[2,96,384]{2,1,0:T(8,128)(2,1)}) custom-call(s32[9]{0:T(128)} %refs_0_.5, bf16[4,96,384]{2,1,0:T(8,128)(2,1)S(1)} %collective-permute-done.2.refs_1_, bf16[4,24,384]{2,1,0:T(8,128)(2,1)S(1)} %collective-permute-done.3.refs_2_, ...), custom_call_target="tpu_custom_call", output_to_operand_aliasing={{0}: (17, {})} | custom-call | tf_op jit(solution)/shard_map/tick1/pallas_call | solution.py:434
Async XLA Ops:
  1.9 9.4 %collective-permute-start = (bf16[8,24,384]{2,1,0:T(8,128)(2,1)S(1)}, bf16[8,24,384]{2,1,0:T(8,128)(2,1)S(1)}, u32[]{:S(2)}, u32[]{:S(2)}) collective-permute-start(bf16[8,24,384]{2,1,0:T(8,128)(2,1)S(1)} %get-tuple-element.33), channel_id=1, source_target_pairs={{0,1},{1,0},{2,3},{3,2},{4,5},{5,4},{6,7},{7,6},{8,9},{9,8},{10,11... | collective-permute-start | bytes 442376 | tf_op jit(solution)/shard_map/ppermute | solution.py:492
  3.5 9.3 %collective-permute-start.1 = (bf16[8,24,384]{2,1,0:T(8,128)(2,1)S(1)}, bf16[8,24,384]{2,1,0:T(8,128)(2,1)S(1)}, u32[]{:S(2)}, u32[]{:S(2)}) collective-permute-start(bf16[8,24,384]{2,1,0:T(8,128)(2,1)S(1)} %get-tuple-element.34), channel_id=1, source_target_pairs={{0,0},{1,2},{2,1},{3,4},{4,3},{5,6},{6,5},{7,8},{8,7},{9,10},{10,9... | collective-permute-start | bytes 442376 | tf_op jit(solution)/shard_map/ppermute | solution.py:492
  24.4 10.4 %collective-permute-start.2 = (bf16[4,96,384]{2,1,0:T(8,128)(2,1)S(1)}, bf16[4,96,384]{2,1,0:T(8,128)(2,1)S(1)}, u32[]{:S(2)}, u32[]{:S(2)}) collective-permute-start(bf16[4,96,384]{2,1,0:T(8,128)(2,1)S(1)} %get-tuple-element.44), channel_id=1, source_target_pairs={{0,16},{1,17},{2,18},{3,19},{4,20},{5,21},{6,22},{7,23},{8,24},{9,... | collective-permute-start | bytes 884744 | tf_op jit(solution)/shard_map/ppermute | solution.py:542
  24.4 6.9 %collective-permute-start.3 = (bf16[4,24,384]{2,1,0:T(8,128)(2,1)S(1)}, bf16[4,24,384]{2,1,0:T(8,128)(2,1)S(1)}, u32[]{:S(2)}, u32[]{:S(2)}) collective-permute-start(bf16[4,24,384]{2,1,0:T(8,128)(2,1)S(1)} %get-tuple-element.45), channel_id=1, source_target_pairs={{0,17},{1,16},{2,19},{3,18},{4,21},{5,20},{6,23},{7,22},{8,25},{9,... | collective-permute-start | bytes 221192 | tf_op jit(solution)/shard_map/ppermute | solution.py:542
  25.0 9.8 %collective-permute-start.4 = (bf16[4,24,384]{2,1,0:T(8,128)(2,1)S(1)}, bf16[4,24,384]{2,1,0:T(8,128)(2,1)S(1)}, u32[]{:S(2)}, u32[]{:S(2)}) collective-permute-start(bf16[4,24,384]{2,1,0:T(8,128)(2,1)S(1)} %get-tuple-element.46), channel_id=1, source_target_pairs={{0,16},{1,18},{2,17},{3,20},{4,19},{5,22},{6,21},{7,24},{8,23},{9,... | collective-permute-start | bytes 221192 | tf_op jit(solution)/shard_map/ppermute | solution.py:542

commit v4 on v3

--- a/solution.py
+++ b/solution.py
@@ -84,42 +84,51 @@
     return v / (1.0 + jnp.exp(-v))
 
 
-def push_weights(weights, a, step, slot):
+def weight_tile(weights, taps, step):
     at = step * TILE
     depth = min(TILE, K - at)
-    left = weights[a, at : at + depth, 0:TILE]
-    right = weights[a, at : at + depth, TILE:C]
-    right = jnp.concatenate([right, right], axis=1)
+    if len(taps) == 1:
+        tile = weights[taps[0], at : at + depth, 0:TILE]
+    else:
+        empty = jnp.zeros((depth, C - TILE), BF16)
+        tile = jnp.concatenate(
+            [empty if a is None else weights[a, at : at + depth, TILE:C] for a in taps], axis=1
+        )
     if depth < TILE:
-        empty = jnp.zeros((TILE - depth, TILE), BF16)
-        left = jnp.concatenate([left, empty], axis=0)
-        right = jnp.concatenate([right, empty], axis=0)
-    pltpu.matmul_push_rhs(left, slot, 0)
-    pltpu.matmul_push_rhs(right, slot, 1)
-
-
-def multiply(accumulators, operand, index, step, slot):
+        tile = jnp.concatenate([tile, jnp.zeros((TILE - depth, TILE), BF16)], axis=0)
+    return tile
+
+
+def multiply(accumulator, operand, index, step, slot):
     at = step * TILE
     depth = min(TILE, K - at)
-    rows = operand[index][:, at : at + depth] if isinstance(operand, list) else operand[index, :, at : at + depth]
+    rows = operand[index, :, at : at + depth]
     if depth < TILE:
         rows = jnp.concatenate([rows, rows], axis=1)
-    for accumulator in accumulators:
-        pltpu.matmul_acc_lhs(accumulator, rows, load_staged_rhs=slot)
-
-
-def popped(accumulators):
-    return jnp.concatenate([pltpu.matmul_pop(accumulators[0]), pltpu.matmul_pop(accumulators[1])[:, : C - TILE]], axis=1)
-
-
-def woven(steps, thunks):
-    order, done = [], 0
-    for i, step in enumerate(steps):
-        order.append(step)
-        due = (i + 1) * len(thunks) // len(steps)
-        order += thunks[done:due]
-        done = due
-    return order
+    pltpu.matmul_acc_lhs(accumulator, rows, load_staged_rhs=slot)
+
+
+def halves(accumulator):
+    both = pltpu.matmul_pop(accumulator)
+    return both[:, : C - TILE], both[:, C - TILE :]
+
+
+def timeline(phases, groups):
+    clock, starts, ends, entries = [0, 0], {}, {}, []
+    for name, units in phases:
+        for unit, steps in enumerate(units):
+            starts[name, unit] = clock[unit]
+            for step in steps:
+                entries.append((clock[unit], 1, len(entries), step))
+                clock[unit] += sum(operand.shape[1] for _, operand, _ in step[4])
+            ends[name, unit] = clock[unit]
+    for after, before, thunks in groups:
+        first = max(ends[after, 0], ends[after, 1]) if after else -1
+        last = min(starts[before, 0], starts[before, 1]) if before else max(clock) + 1
+        last = max(last, first + 1)
+        for i, thunk in enumerate(thunks):
+            entries.append((first + (last - first) * i / len(thunks), 0, len(entries), thunk))
+    return [entry[3] for entry in sorted(entries, key=lambda entry: entry[:3])]
 
 
 def first_normed(frame, keep, gain):
@@ -127,14 +136,16 @@
 
 
 class Section:
-    def __init__(self, refs, accumulators, live, even, at_top, at_bottom):
+    def __init__(self, refs, accumulators, even, at_top, at_bottom):
         self.__dict__.update(refs)
-        self.live, self.even, self.at_top, self.at_bottom = live, even, at_top, at_bottom
-        frames = FRAMES
-        self.sums1 = [(accumulators[f], accumulators[frames + f]) for f in range(frames)]
-        self.sums2 = [(accumulators[2 * frames + f], accumulators[3 * frames + f]) for f in range(frames)]
-        at = 4 * frames
-        self.edges1 = [(accumulators[at + i], accumulators[at + 2 + i]) for i in range(2)]
+        self.even, self.at_top, self.at_bottom = even, at_top, at_bottom
+        at = 0
+        for name, (_, _, count) in ACCUMULATORS.items():
+            setattr(self, name, accumulators[at : at + count])
+            at += count
+        self.left = [self.left[:4], self.left[:2] + self.left[4:]]
+        self.right = [self.right[:5], self.right[:3] + self.right[5:] + self.right[4:5]]
+        self.saved = None
 
     def halo(self, f):
         near, far = self.near[f].astype(F32), self.far[f].astype(F32)
@@ -143,13 +154,11 @@
         return top, bottom
 
     def norm_first(self, f):
-        self.window1[f + 2] = first_normed(self.x[f], f < self.live, self.gain1[...])
+        self.window1[f + 2] = normed(self.x[f].astype(F32), self.gain1[...]).astype(BF16)
 
     def norm_first_halo(self, f):
-        keep = f < self.live
         gain = self.gain1[...]
-        top, bottom = (jnp.where(keep, rows, 0.0) for rows in self.halo(f))
-        values = jnp.concatenate([top, bottom], axis=0)
+        values = jnp.concatenate(self.halo(f), axis=0)
         self.halos[f + 2] = normed(values, gain).astype(BF16)
 
     def build_first_edges(self, g):
@@ -205,66 +214,100 @@
         out += [lambda g=g, b=b: self.build_second(g, b) for g in (pair, pair + 1) for b in range(3)]
         return out
 
+    def pop_sums(self, conv, f):
+        left = pltpu.matmul_pop(self.left[conv][f])
+        if f < 2 and conv in self.moved:
+            left = left + pltpu.matmul_pop(self.moved_left[f])
+        if f == 0:
+            self.saved = halves(self.right[conv][0])[0] if self.early1 is None else 0.0
+        right, (following, second) = self.saved, halves(self.right[conv][f + 1])
+        self.saved = following
+        sums = jnp.concatenate([left, right + second], axis=1)
+        if self.early1 is not None and f < 2:
+            sums = sums + (self.early1, self.early2)[conv][f]
+        return sums
+
+    def pop_edges(self, i):
+        left = pltpu.matmul_pop(self.left_edges[i])
+        if i == 0 and 0 in self.moved:
+            left = left + pltpu.matmul_pop(self.moved_edges[0])
+        if i or self.early1 is None:
+            right = halves(self.right_edges[i])[0] + halves(self.right_edges[2 + i])[1]
+        else:
+            right = halves(self.right_edges[2])[1]
+        sums = jnp.concatenate([left, right], axis=1)
+        return sums + self.early_edges[...] if self.early1 is not None and i == 0 else sums
+
     def norm_second(self, f):
-        hidden = popped(self.sums1[f]) + self.bias1[...]
-        if self.early1 is not None and f < 2:
-            hidden = hidden + self.early1[f]
-        hidden = jnp.where(f < self.live, hidden, 0.0)
+        hidden = jnp.where(f < self.live(), self.pop_sums(0, f) + self.bias1[...], 0.0)
         self.window2[f + 2] = normed(hidden, self.gain2[...]).astype(BF16)
 
     def norm_second_edges(self, i):
-        hidden = popped(self.edges1[i]) + self.bias1[...]
-        if self.early1 is not None and i == 0:
-            hidden = hidden + self.early_edges[...]
+        hidden = self.pop_edges(i) + self.bias1[...]
         place = lax.broadcasted_iota(jnp.int32, (2 * EDGE, C), 0)
         outside = ((place % 2 == 0) & self.at_top) | ((place % 2 == 1) & self.at_bottom)
         hidden = jnp.where(outside, 0.0, hidden)
         values = normed(hidden, self.gain2[...]).astype(BF16).astype(F32)
         for j in range(2):
             f = 2 * i + j
-            self.hidden_edges[f + 2] = jnp.where(f < self.live, values[j * EDGE : (j + 1) * EDGE], 0.0)
+            self.hidden_edges[f + 2] = jnp.where(f < self.live(), values[j * EDGE : (j + 1) * EDGE], 0.0)
 
     def final(self, f):
-        result = popped(self.sums2[f]) + self.bias2[...] + self.x[f].astype(F32)
-        if self.early1 is not None and f < 2:
-            result = result + self.early2[f]
-        return jnp.where(f < self.live, result, 0.0).astype(BF16)
+        result = self.pop_sums(1, f) + self.bias2[...] + self.x[f].astype(F32)
+        return jnp.where(f < self.live(), result, 0.0).astype(BF16)
 
     def phase(self, conv, pair):
         weights = (self.weights1, self.weights2)[conv]
         operand = (self.operand1, self.operand2)[conv]
-        sums = (self.sums1, self.sums2)[conv]
-        steps = []
+        moved = conv in self.moved
+        units = ([], [])
+
+        def add(unit, taps, work, edge_work=()):
+            work = [(accumulator, operand, g) for accumulator, g in work]
+            if conv == 0:
+                work += [(accumulator, self.edges, g) for accumulator, g in edge_work]
+            units[unit].extend((unit, taps, step, weights, work) for step in range(STEPS))
+
+        left, right = self.left[conv], self.right[conv]
         for a in range(3):
-            work = [(sums[g - a], operand, g) for g in (pair, pair + 1) if 0 <= g - a < FRAMES]
-            if conv == 0:
-                for i in range(2):
-                    if pair <= 2 * i + a + 1 < pair + 2:
-                        work.append((self.edges1[i], self.edges, 2 * i + a))
-            if work:
-                steps += [(conv, a, step, weights, work) for step in range(STEPS)]
-        return steps
+            work = [(left[g - a], g) for g in (pair, pair + 1) if 0 <= g - a < FRAMES]
+            edge_work = [(self.left_edges[i], 2 * i + a) for i in range(2) if pair <= 2 * i + a + 1 < pair + 2]
+            if moved and pair == 2 and a == 2:
+                work = [(self.moved_left[f], f + 2) for f in range(2)]
+                add(1, (2,), work, [(self.moved_edges[0], 2)])
+            elif work:
+                add(0, (a,), work, edge_work)
+        edges = self.right_edges
+        if pair == 0:
+            add(1, (0, 1), [(right[0], 0), (right[1], 1)], [(edges[0], 0)])
+        elif pair == 2:
+            add(1, (0, 1), [(right[2], 2), (right[3], 3)], [(edges[2], 1), (edges[1], 2)])
+            add(1, (None, 2), [(right[1], 2), (right[2], 3)], [(edges[2], 2)])
+        else:
+            add(1, (1, 2), [(right[3], 4), (right[4], 5)], [(edges[1], 3), (edges[3], 4)])
+        return (conv, pair), units
 
     def run(self, order):
-        steps = [entry for entry in order if isinstance(entry, tuple)]
-
-        def push(i):
-            _, a, step, weights, _ = steps[i]
-            push_weights(weights, a, step, i % 2)
-
-        i = 0
+        steps = [[entry for entry in order if isinstance(entry, tuple) and entry[0] == unit] for unit in range(2)]
+        count = [0, 0]
+
+        def push(unit, i):
+            _, taps, step, weights, _ = steps[unit][i]
+            pltpu.matmul_push_rhs(weight_tile(weights, taps, step), i % 2, unit)
+
         for entry in order:
             if not isinstance(entry, tuple):
                 entry()
                 continue
+            unit, _, step, _, work = entry
+            i = count[unit]
+            count[unit] += 1
             if i == 0:
-                push(0)
-            if i + 1 < len(steps):
-                push(i + 1)
-            _, _, step, _, work = entry
-            for n, (accumulators, operand, g) in enumerate(work):
-                multiply(accumulators, operand, g, step, i % 2 if n == 0 else None)
-            i += 1
+                push(unit, 0)
+            if i + 1 < len(steps[unit]):
+                push(unit, i + 1)
+            for n, (accumulator, operand, g) in enumerate(work):
+                multiply(accumulator, operand, g, step, i % 2 if n == 0 else None)
 
 
 def edges_out(main, even, near, far, f):
@@ -273,11 +316,18 @@
     far[f] = jnp.where(even, upper, lower).astype(BF16)
 
 
-def pack_kernel(x, first, second, near, far):
+def pack_kernel(counts_hbm, x, first, second, near, far, counts, sem):
+    counting = pltpu.make_async_copy(counts_hbm, counts, sem)
+    counting.start()
     even = lax.axis_index("strip") % 2 == 0
-    for source, start in ((x, 0), (first, 4), (second, 6)):
+    for source, start in ((first, 4), (second, 6), (x, 0)):
+        if start == 0:
+            counting.wait()
         for f in range(source.shape[0]):
-            edges_out(source[f].astype(F32), even, near, far, start + f)
+            rows = source[f].astype(F32)
+            if start == 0:
+                rows = jnp.where(f < live_frames(counts, 0), rows, 0.0)
+            edges_out(rows, even, near, far, start + f)
 
 
 WINDOW = (FRAMES + 2, MAIN, C)
@@ -294,16 +344,25 @@
     return counts[7 - lax.axis_index("segment") + tick]
 
 
-def with_section(given, live, body):
+ACCUMULATORS = dict(
+    left=(0, MAIN, FRAMES + 2),
+    left_edges=(0, 2 * EDGE, 2),
+    right=(1, MAIN, FRAMES + 2),
+    right_edges=(1, 2 * EDGE, 4),
+    moved_left=(1, MAIN, 2),
+    moved_edges=(1, 2 * EDGE, 1),
+)
+
+
+def with_section(given, body):
     strip = lax.axis_index("strip")
     given = {"early1": None, **given}
 
     def inner(*accumulators):
-        body(Section(given, accumulators, live, strip % 2 == 0, strip == 0, strip == lax.axis_size("strip") - 1))
-
-    shapes = [MAIN] * (4 * FRAMES) + [2 * EDGE] * 4
-    units = ([0] * FRAMES + [1] * FRAMES) * 2 + [0, 0, 1, 1]
-    pl.run_scoped(inner, *[pltpu.ACC(unit)((rows, TILE), F32) for unit, rows in zip(units, shapes)])
+        body(Section(given, accumulators, strip % 2 == 0, strip == 0, strip == lax.axis_size("strip") - 1))
+
+    shapes = [pltpu.ACC(unit)((rows, TILE), F32) for unit, rows, count in ACCUMULATORS.values() for _ in range(count)]
+    pl.run_scoped(inner, *shapes)
 
 
 def prepare_kernel(r):
@@ -331,33 +390,41 @@
     copies = [pltpu.make_async_copy(r["weights2_hbm"].at[a], r["weights2"].at[a], r["sems"].at[a]) for a in range(3)]
     for copy in copies:
         copy.start()
-    counting.wait()
-    live = live_frames(r["counts"], 0)
 
     def body(work):
         work.norms = False
+        work.moved = (0, 1)
+        work.live = lambda: live_frames(r["counts"], 0)
         work.window2[0:2] = work.second[...]
         for g in range(2):
             work.halos[g] = jnp.concatenate(work.halo(4 + g), axis=0).astype(BF16)
             work.hidden_edges[g] = edge_pair(*work.halo(6 + g))
-        order = work.first_thunks(0, cached=True)
-        order += woven(work.phase(0, 0), work.first_thunks(2))
-        order += woven(work.phase(0, 2), work.first_thunks(4) + work.second_thunks(0, cached=True))
-        order += woven(work.phase(0, 4), work.second_thunks(2))
-        at = max(i for i, entry in enumerate(order) if isinstance(entry, tuple))
-        order[at:at] = [copy.wait for copy in copies]
-        order += woven(work.phase(1, 0), work.second_thunks(4))
-        order += work.phase(1, 2) + work.phase(1, 4)
-        work.run(order)
         last = lax.axis_index("segment") == lax.axis_size("segment") - 1
-        for f in range(FRAMES):
+
+        def finish(f):
             result = work.final(f)
             work.result[f] = result
-            passed = jnp.where(last, work.incoming[f].astype(F32), result.astype(F32))
+            fresh = jnp.where(f < r["counts"][8], work.incoming[f].astype(F32), 0.0)
+            passed = jnp.where(last, fresh, result.astype(F32))
             work.send[f] = passed.astype(BF16)
             edges_out(passed, work.even, work.send_near, work.send_far, f)
 
-    with_section(r, live, body)
+        finishing = [lambda f=f: finish(f) for f in range(FRAMES)]
+        phases = [work.phase(conv, pair) for conv in range(2) for pair in (0, 2, 4)]
+        groups = [
+            (None, (0, 0), work.first_thunks(0, cached=True)),
+            (None, (0, 2), work.first_thunks(2)),
+            ((0, 0), (0, 4), work.first_thunks(4)),
+            ((0, 0), (0, 4), work.second_thunks(0, cached=True)),
+            ((0, 0), (0, 4), [counting.wait]),
+            ((0, 2), (1, 0), [copy.wait for copy in copies]),
+            ((0, 2), (1, 0), work.second_thunks(2)),
+            ((0, 4), (1, 2), work.second_thunks(4)),
+            ((1, 2), None, finishing[:2]),
+        ]
+        work.run(timeline(phases, groups) + finishing[2:])
+
+    with_section(r, body)
 
 
 def between_kernel(r):
@@ -374,25 +441,34 @@
         r["second_edge"][i] = r["edges_old"][live + i]
 
     def body(work):
+        work.moved = ()
+
+        def store(conv, sums):
+            for f in range(2):
+                right, second = halves(work.right[conv][f])
+                if f == 1:
+                    sums[0, :, TILE:C] += second
+                sums[f, :, 0:TILE] = pltpu.matmul_pop(work.left[conv][f])
+                sums[f, :, TILE:C] = right
+            if conv == 0:
+                work.sum_edges[:, 0:TILE] = pltpu.matmul_pop(work.left_edges[0])
+                work.sum_edges[:, TILE:C] = halves(work.right_edges[0])[0]
+
         order = work.first_thunks(0, cached=True)
-        order += woven(work.phase(0, 0), work.second_thunks(0, cached=True))
-        order += work.phase(1, 0)
+        order += timeline([work.phase(0, 0)], [(None, None, work.second_thunks(0, cached=True))])
+        order += [lambda: store(0, work.sum1)]
+        order += timeline([work.phase(1, 0)], [])
         work.run(order)
-        for f in range(2):
-            work.sum1[f] = popped(work.sums1[f])
-            work.sum2[f] = popped(work.sums2[f])
-        work.sum_edges[...] = popped(work.edges1[0])
+        store(1, work.sum2)
 
     given = dict(r, window1=r["first"], halos=r["first_halo"], window2=r["second"], hidden_edges=r["second_edge"])
-    with_section(given, live, body)
+    with_section(given, body)
     writing.wait()
 
 
 def tick1_kernel(r):
     counting = pltpu.make_async_copy(r["counts_hbm"], r["counts"], r["sems"].at[0])
     counting.start()
-    counting.wait()
-    live = live_frames(r["counts"], 1)
     copies = []
 
     def send(source, target):
@@ -401,26 +477,37 @@
 
     def body(work):
         work.norms = True
+        work.moved = (1,)
+        work.live = lambda: live_frames(r["counts"], 1)
         for i in range(2):
             work.window1[i] = work.first[i]
             work.halos[i] = work.first_halo[i]
             work.window2[i] = work.second[i]
             work.hidden_edges[i] = work.second_edge[i]
-        order = [lambda: work.build_first_edges(1)] + work.first_thunks(2)
-        order += woven(work.phase(0, 2), work.first_thunks(4))
-        order += [lambda: send(work.window1.at[pl.ds(live, 2)], work.first_next)]
-        order += woven(work.phase(0, 4), work.second_thunks(2))
-        order += woven(work.phase(1, 2), work.second_thunks(4))
-        order += [lambda: send(work.window2.at[pl.ds(live, 2)], work.second_next)]
-        order += work.phase(1, 4)
-        work.run(order)
-        for f in range(FRAMES):
+
+        def finish(f):
             work.result[f] = work.final(f)
             send(work.result.at[f], work.whole.at[1, f])
+
+        def send_window(window, target):
+            send(window.at[pl.ds(work.live(), 2)], target)
+
+        finishing = [lambda f=f: finish(f) for f in range(FRAMES)]
+        phases = [work.phase(conv, pair) for conv in range(2) for pair in (2, 4)]
+        groups = [
+            (None, (0, 4), work.first_thunks(4)),
+            (None, (0, 4), [counting.wait]),
+            ((0, 2), (1, 2), work.second_thunks(2)),
+            ((0, 2), (1, 2), [lambda: send_window(work.window1, work.first_next)]),
+            ((0, 4), (1, 4), work.second_thunks(4)),
+            ((1, 2), None, finishing[:2]),
+        ]
+        order = [lambda: work.build_first_edges(1)] + work.first_thunks(2) + timeline(phases, groups)
+        work.run(order + [lambda: send_window(work.window2, work.second_next)] + finishing[2:])
         for copy in copies:
             copy.wait()
 
-    with_section(r, live, body)
+    with_section(r, body)
 
 
 def call(kernel, operands, outputs, scratch, flops=0, moved=0):
@@ -474,22 +561,31 @@
 ):
     segments = lax.axis_size("segment")
     strips = lax.axis_size("strip")
-    swaps = [
-        [(i, i ^ 1) for i in range(strips)],
-        [(i, i if i in (0, strips - 1) else ((i + 1) ^ 1) - 1) for i in range(strips)],
-    ]
+    axes = ("segment", "strip")
+
+    def swap(rows, far, step):
+        pairs = []
+        for s in range(segments):
+            for k in range(strips):
+                to, into = (((k + 1) ^ 1) - 1 if far else k ^ 1), (s + step) % segments
+                if not 0 <= to < strips:
+                    to, into = k, (into if step else s ^ 1)
+                pairs.append((s * strips + k, into * strips + to))
+        return lax.ppermute(rows, axes, pairs)
+
     x = flat(held_blocks[0])
     first = flat(first_cache[0])
     second = flat(second_cache[0])
     near, far = pl.pallas_call(
         pack_kernel,
         out_shape=[pltpu.VMEM((8, EDGE, C), BF16)] * 2,
-        in_specs=[VMEM] * 3,
+        in_specs=[HBM] + [VMEM] * 3,
         out_specs=[VMEM] * 2,
+        scratch_shapes=[pltpu.SMEM((9,), jnp.int32), pltpu.SemaphoreType.DMA],
         compiler_params=pltpu.CompilerParams(vmem_limit_bytes=8 << 20),
         name="pack",
-    )(*(pltpu.with_memory_space_constraint(rows, pltpu.HBM) for rows in (x, first, second)))
-    near, far = (lax.ppermute(rows, "strip", swap) for rows, swap in zip((near, far), swaps))
+    )(*(pltpu.with_memory_space_constraint(rows, pltpu.HBM) for rows in (frame_counts, x, first, second)))
+    near, far = swap(near, False, 0), swap(far, True, 0)
     counts = dict(counts_hbm=frame_counts)
     count_scratch = dict(counts=pltpu.SMEM((9,), jnp.int32), sems=pltpu.SemaphoreType.DMA((16,)))
     block = pltpu.VMEM((FRAMES, MAIN, C), BF16)
@@ -537,12 +633,9 @@
         {**OPERANDS, **count_scratch},
     )
 
-    def onward(rows, swap):
-        pairs = [(s * strips + i, (s + 1) % segments * strips + j) for s in range(segments) for i, j in swap]
-        return lax.ppermute(rows, ("segment", "strip"), pairs)
-
-    x = onward(done["send"], [(i, i) for i in range(strips)])
-    near, far = (onward(done[n], swap) for n, swap in zip(("send_near", "send_far"), swaps))
+    onward = [(s * strips + k, (s + 1) % segments * strips + k) for s in range(segments) for k in range(strips)]
+    x = lax.ppermute(done["send"], axes, onward)
+    near, far = swap(done["send_near"], False, 1), swap(done["send_far"], True, 1)
     both = dict(weights1=ready["weights1"], weights2=done["weights2"])
     early = call(
         between_kernel,

time: 44.9 us -> 40.1 us (0.89)
  Pallas kernels: 30.1 us -> 27.2 us
  starting transfers between devices: 8.81 us -> 6.91 us
    pallas_call x4, Pallas kernels: 28.9 us -> 25.3 us  [call(): pl.pallas_call(lambda *refs: kernel(dict(zip(names, refs))), out_shape=li...]
    ppermute x5, starting transfers between devices: 8.81 us -> 6.91 us  [the longest x4 6.9 us: swap(): return lax.ppermute(rows, axes, pairs)]
    pallas_call x1, Pallas kernels: 1.26 us -> 1.87 us  [on_device(): pl.pallas_call(pack_kernel, out_shape=[pltpu.VMEM((8, EDGE, C), BF16)] *...]
  transfers between devices with their start and end apart: 5 -> 5, of which waited for: 2 -> 2; matrix products, arithmetic and copies ran while one was open for 0% -> 0% of each run, Pallas kernels for 17% -> 19%
where the time goes in v4:
time: 40.1 us; the launch traced here: 40 us
  Pallas kernels  27.2 us (68%)
  starting transfers between devices  6.91 us (17%)
  waiting for transfers between devices  5.06 us (13%)
  between operations  0.84 us (2%)
    pallas_call x4, Pallas kernels, call(): pl.pallas_call(lambda *refs: kernel(dict(zip(names, refs))), out_shape=li...  25.3 us
    ppermute x4, starting transfers between devices, swap(): return lax.ppermute(rows, axes, pairs)  6.9 us
    ppermute x4, waiting for transfers between devices, swap(): return lax.ppermute(rows, axes, pairs)  5.06 us
    pallas_call x1, Pallas kernels, on_device(): pl.pallas_call(pack_kernel, out_shape=[pltpu.VMEM((8, EDGE, C), BF16)] *...  1.87 us
  transfers between devices with their start and end apart: 5, of which 2 were waited for; matrix products, arithmetic and copies ran while one was open for 0% of the time, Pallas kernels for 19%

profile of v4, /device:TPU:96, one launch (start us, length us, event | category | flops | bytes accessed | tf_op | source)
XLA Modules:
  0.0 40.0 jit_solution(15915623825167303615)
XLA Ops:
  0.6 1.9 %pack.1 = (bf16[8,24,384]{2,1,0:T(8,128)(2,1)S(1)}, bf16[8,24,384]{2,1,0:T(8,128)(2,1)S(1)}) custom-call(s32[9]{0:T(128)} %refs_0_.5, bf16[4,96,384]{2,1,0:T(8,128)(2,1)} %bitcast.39, bf16[2,96,384]{2,1,0:T(8,128)(2,1)} %bitcast.42, bf16[2,96,384]{2,1,0:T(8,128)(2,1)} %bitcast.44), custom_call_target="tpu_custom_call" | custom-call | tf_op jit(solution)/shard_map/pack/pallas_call | solution.py:579
  2.5 1.7 %collective-permute-start = (bf16[8,24,384]{2,1,0:T(8,128)(2,1)S(1)}, bf16[8,24,384]{2,1,0:T(8,128)(2,1)S(1)}, u32[]{:S(2)}, u32[]{:S(2)}) collective-permute-start(bf16[8,24,384]{2,1,0:T(8,128)(2,1)S(1)} %get-tuple-element.33), channel_id=1, source_target_pairs={{0,1},{1,0},{2,3},{3,2},{4,5},{5,4},{6,7},{7,6},{8,9},{9,8},{10,11... | collective-permute-start | bytes 442376 | tf_op jit(solution)/shard_map/ppermute | solution.py:574
  4.2 2.0 %collective-permute-start.1 = (bf16[8,24,384]{2,1,0:T(8,128)(2,1)S(1)}, bf16[8,24,384]{2,1,0:T(8,128)(2,1)S(1)}, u32[]{:S(2)}, u32[]{:S(2)}) collective-permute-start(bf16[8,24,384]{2,1,0:T(8,128)(2,1)S(1)} %get-tuple-element.34), channel_id=1, source_target_pairs={{0,16},{1,2},{2,1},{3,4},{4,3},{5,6},{6,5},{7,8},{8,7},{9,10},{10,... | collective-permute-start | bytes 442376 | tf_op jit(solution)/shard_map/ppermute | solution.py:574
  6.2 3.8 %prepare.1 = (bf16[4,96,384]{2,1,0:T(8,128)(2,1)S(1)}, bf16[2,96,384]{2,1,0:T(8,128)(2,1)S(1)}, bf16[4,96,384]{2,1,0:T(8,128)(2,1)S(1)}, bf16[6,96,384]{2,1,0:T(...) custom-call(bf16[4,96,384]{2,1,0:T(8,128)(2,1)} %bitcast.40, ...), custom_call_target="tpu_custom_call" | custom-call | bytes 7962624 | tf_op jit(solution)/shard_map/prepare/pallas_call | solution.py:521
  10.0 0.0 collective-permute-done.refs_1_
  10.0 1.5 %collective-permute-done.1.refs_2_ = bf16[8,24,384]{2,1,0:T(8,128)(2,1)S(1)} collective-permute-done((bf16[8,24,384]{2,1,0:T(8,128)(2,1)S(1)}, bf16[8,24,384]{2,1,0:T(8,128)(2,1)S(1)}, u32[]{:S(2)}, u32[]{:S(2)}) %collective-permute-start.1) | collective-permute-done | bytes 147488 | tf_op jit(solution)/shard_map/ppermute | solution.py:574
  11.6 9.3 %tick0.1 = (bf16[3,3456,384]{2,1,0:T(8,128)(2,1)S(1)}, bf16[6,48,384]{2,1,0:T(8,128)(2,1)S(1)}, bf16[6,96,384]{2,1,0:T(8,128)(2,1)S(1)}, f32[6,24,384]{2,1,0:T(8...) custom-call(s32[9]{0:T(128)} %refs_0_.5, ...), custom_call_target="tpu_custom_call" | custom-call | tf_op jit(solution)/shard_map/tick0/pallas_call | solution.py:521
  20.9 0.0 collective-permute-start.2
  20.9 0.5 %collective-permute-start.3 = (bf16[4,24,384]{2,1,0:T(8,128)(2,1)S(1)}, bf16[4,24,384]{2,1,0:T(8,128)(2,1)S(1)}, u32[]{:S(2)}, u32[]{:S(2)}) collective-permute-start(bf16[4,24,384]{2,1,0:T(8,128)(2,1)S(1)} %get-tuple-element.45), channel_id=1, source_target_pairs={{0,17},{1,16},{2,19},{3,18},{4,21},{5,20},{6,23},{7,22},{8,25},{9,... | collective-permute-start | bytes 221192 | tf_op jit(solution)/shard_map/ppermute | solution.py:574
  21.4 2.7 %collective-permute-start.4 = (bf16[4,24,384]{2,1,0:T(8,128)(2,1)S(1)}, bf16[4,24,384]{2,1,0:T(8,128)(2,1)S(1)}, u32[]{:S(2)}, u32[]{:S(2)}) collective-permute-start(bf16[4,24,384]{2,1,0:T(8,128)(2,1)S(1)} %get-tuple-element.46), channel_id=1, source_target_pairs={{0,16},{1,18},{2,17},{3,20},{4,19},{5,22},{6,21},{7,24},{8,23},{9,... | collective-permute-start | bytes 221192 | tf_op jit(solution)/shard_map/ppermute | solution.py:574
  24.1 3.6 %between.1 = (bf16[2,4,96,384]{3,2,1,0:T(8,128)(2,1)}, bf16[2,96,384]{2,1,0:T(8,128)(2,1)S(1)}, bf16[2,48,384]{2,1,0:T(8,128)(2,1)S(1)}, bf16[2,96,384]{2,1,0:T(...) custom-call(s32[9]{0:T(128)} %refs_0_.5, ...), custom_call_target="tpu_custom_call" | custom-call | flops 1528823808 | bytes 7962624 | tf_op jit(solution)/shard_map/between/pallas_call | solution.py:521
  27.8 0.0 collective-permute-done.3.refs_2_
  27.8 3.5 %collective-permute-done.4.refs_3_ = bf16[4,24,384]{2,1,0:T(8,128)(2,1)S(1)} collective-permute-done((bf16[4,24,384]{2,1,0:T(8,128)(2,1)S(1)}, bf16[4,24,384]{2,1,0:T(8,128)(2,1)S(1)}, u32[]{:S(2)}, u32[]{:S(2)}) %collective-permute-start.4) | collective-permute-done | bytes 73760 | tf_op jit(solution)/shard_map/ppermute | solution.py:574
  31.3 0.0 collective-permute-done.2.refs_1_
  31.3 8.5 %tick1.1 = (bf16[2,4,96,384]{3,2,1,0:T(8,128)(2,1)}, bf16[2,96,384]{2,1,0:T(8,128)(2,1)}, bf16[2,96,384]{2,1,0:T(8,128)(2,1)}) custom-call(s32[9]{0:T(128)} %refs_0_.5, bf16[4,96,384]{2,1,0:T(8,128)(2,1)S(1)} %collective-permute-done.2.refs_1_, bf16[4,24,384]{2,1,0:T(8,128)(2,1)S(1)} %collective-permute-done.3.refs_2_, ...), custom_call_target="tpu_custom_call", output_to_operand_aliasing={{0}: (17, {})} | custom-call | tf_op jit(solution)/shard_map/tick1/pallas_call | solution.py:521
Async XLA Ops:
  2.5 7.5 %collective-permute-start = (bf16[8,24,384]{2,1,0:T(8,128)(2,1)S(1)}, bf16[8,24,384]{2,1,0:T(8,128)(2,1)S(1)}, u32[]{:S(2)}, u32[]{:S(2)}) collective-permute-start(bf16[8,24,384]{2,1,0:T(8,128)(2,1)S(1)} %get-tuple-element.33), channel_id=1, source_target_pairs={{0,1},{1,0},{2,3},{3,2},{4,5},{5,4},{6,7},{7,6},{8,9},{9,8},{10,11... | collective-permute-start | bytes 442376 | tf_op jit(solution)/shard_map/ppermute | solution.py:574
  4.2 7.4 %collective-permute-start.1 = (bf16[8,24,384]{2,1,0:T(8,128)(2,1)S(1)}, bf16[8,24,384]{2,1,0:T(8,128)(2,1)S(1)}, u32[]{:S(2)}, u32[]{:S(2)}) collective-permute-start(bf16[8,24,384]{2,1,0:T(8,128)(2,1)S(1)} %get-tuple-element.34), channel_id=1, source_target_pairs={{0,16},{1,2},{2,1},{3,4},{4,3},{5,6},{6,5},{7,8},{8,7},{9,10},{10,... | collective-permute-start | bytes 442376 | tf_op jit(solution)/shard_map/ppermute | solution.py:574
  20.9 10.4 %collective-permute-start.2 = (bf16[4,96,384]{2,1,0:T(8,128)(2,1)S(1)}, bf16[4,96,384]{2,1,0:T(8,128)(2,1)S(1)}, u32[]{:S(2)}, u32[]{:S(2)}) collective-permute-start(bf16[4,96,384]{2,1,0:T(8,128)(2,1)S(1)} %get-tuple-element.44), channel_id=1, source_target_pairs={{0,16},{1,17},{2,18},{3,19},{4,20},{5,21},{6,22},{7,23},{8,24},{9,... | collective-permute-start | bytes 884744 | tf_op jit(solution)/shard_map/ppermute | solution.py:637
  20.9 6.9 %collective-permute-start.3 = (bf16[4,24,384]{2,1,0:T(8,128)(2,1)S(1)}, bf16[4,24,384]{2,1,0:T(8,128)(2,1)S(1)}, u32[]{:S(2)}, u32[]{:S(2)}) collective-permute-start(bf16[4,24,384]{2,1,0:T(8,128)(2,1)S(1)} %get-tuple-element.45), channel_id=1, source_target_pairs={{0,17},{1,16},{2,19},{3,18},{4,21},{5,20},{6,23},{7,22},{8,25},{9,... | collective-permute-start | bytes 221192 | tf_op jit(solution)/shard_map/ppermute | solution.py:574
  21.4 9.9 %collective-permute-start.4 = (bf16[4,24,384]{2,1,0:T(8,128)(2,1)S(1)}, bf16[4,24,384]{2,1,0:T(8,128)(2,1)S(1)}, u32[]{:S(2)}, u32[]{:S(2)}) collective-permute-start(bf16[4,24,384]{2,1,0:T(8,128)(2,1)S(1)} %get-tuple-element.46), channel_id=1, source_target_pairs={{0,16},{1,18},{2,17},{3,20},{4,19},{5,22},{6,21},{7,24},{8,23},{9,... | collective-permute-start | bytes 221192 | tf_op jit(solution)/shard_map/ppermute | solution.py:574

commit v5 on v4

--- a/solution.py
+++ b/solution.py
@@ -73,9 +73,12 @@
     ]
 
 
+def merged(even, odd):
+    return jnp.where(lax.broadcasted_iota(jnp.int32, (EDGE, C), 0) % 2 == 0, even, odd)
+
+
 def edge_pair(top, bottom):
-    even = lax.broadcasted_iota(jnp.int32, (EDGE, C), 0) % 2 == 0
-    return jnp.where(even, rolled(top, -1, 0), rolled(bottom, 1, 0))
+    return merged(rolled(top, -1, 0), rolled(bottom, 1, 0))
 
 
 def normed(values, gain):
@@ -88,11 +91,11 @@
     at = step * TILE
     depth = min(TILE, K - at)
     if len(taps) == 1:
-        tile = weights[taps[0], at : at + depth, 0:TILE]
+        tile = weights[taps[0]][at : at + depth, 0:TILE]
     else:
         empty = jnp.zeros((depth, C - TILE), BF16)
         tile = jnp.concatenate(
-            [empty if a is None else weights[a, at : at + depth, TILE:C] for a in taps], axis=1
+            [empty if a is None else weights[a][at : at + depth, TILE:C] for a in taps], axis=1
         )
     if depth < TILE:
         tile = jnp.concatenate([tile, jnp.zeros((TILE - depth, TILE), BF16)], axis=0)
@@ -125,7 +128,7 @@
     for after, before, thunks in groups:
         first = max(ends[after, 0], ends[after, 1]) if after else -1
         last = min(starts[before, 0], starts[before, 1]) if before else max(clock) + 1
-        last = max(last, first + 1)
+        last = max(last, first + 0.5)
         for i, thunk in enumerate(thunks):
             entries.append((first + (last - first) * i / len(thunks), 0, len(entries), thunk))
     return [entry[3] for entry in sorted(entries, key=lambda entry: entry[:3])]
@@ -159,6 +162,8 @@
     def norm_first_halo(self, f):
         gain = self.gain1[...]
         values = jnp.concatenate(self.halo(f), axis=0)
+        if not self.norms:
+            values = jnp.where(f < self.live(), values, 0.0)
         self.halos[f + 2] = normed(values, gain).astype(BF16)
 
     def build_first_edges(self, g):
@@ -257,7 +262,10 @@
         return jnp.where(f < self.live(), result, 0.0).astype(BF16)
 
     def phase(self, conv, pair):
-        weights = (self.weights1, self.weights2)[conv]
+        if conv == 0:
+            weights = [self.weights1.at[0], self.weights1.at[1], self.weights1_last]
+        else:
+            weights = [self.weights2.at[a] for a in range(3)]
         operand = (self.operand1, self.operand2)[conv]
         moved = conv in self.moved
         units = ([], [])
@@ -272,10 +280,7 @@
         for a in range(3):
             work = [(left[g - a], g) for g in (pair, pair + 1) if 0 <= g - a < FRAMES]
             edge_work = [(self.left_edges[i], 2 * i + a) for i in range(2) if pair <= 2 * i + a + 1 < pair + 2]
-            if moved and pair == 2 and a == 2:
-                work = [(self.moved_left[f], f + 2) for f in range(2)]
-                add(1, (2,), work, [(self.moved_edges[0], 2)])
-            elif work:
+            if work and not (moved and pair == 2 and a == 2):
                 add(0, (a,), work, edge_work)
         edges = self.right_edges
         if pair == 0:
@@ -283,6 +288,8 @@
         elif pair == 2:
             add(1, (0, 1), [(right[2], 2), (right[3], 3)], [(edges[2], 1), (edges[1], 2)])
             add(1, (None, 2), [(right[1], 2), (right[2], 3)], [(edges[2], 2)])
+            if moved:
+                add(1, (2,), [(self.moved_left[f], f + 2) for f in range(2)], [(self.moved_edges[0], 2)])
         else:
             add(1, (1, 2), [(right[3], 4), (right[4], 5)], [(edges[1], 3), (edges[3], 4)])
         return (conv, pair), units
@@ -310,24 +317,25 @@
                 multiply(accumulator, operand, g, step, i % 2 if n == 0 else None)
 
 
-def edges_out(main, even, near, far, f):
-    upper, lower = rows_out(main, 0), rows_out(main, 6)
+def hand_out(upper, lower, even, near, far, f):
     near[f] = jnp.where(even, lower, upper).astype(BF16)
     far[f] = jnp.where(even, upper, lower).astype(BF16)
 
 
-def pack_kernel(counts_hbm, x, first, second, near, far, counts, sem):
-    counting = pltpu.make_async_copy(counts_hbm, counts, sem)
-    counting.start()
+def edges_out(main, even, near, far, f):
+    hand_out(rows_out(main, 0), rows_out(main, 6), even, near, far, f)
+
+
+def pack_kernel(x, first, second, near, far):
     even = lax.axis_index("strip") % 2 == 0
-    for source, start in ((first, 4), (second, 6), (x, 0)):
-        if start == 0:
-            counting.wait()
+    for source, start in ((first, 4), (x, 0)):
         for f in range(source.shape[0]):
-            rows = source[f].astype(F32)
-            if start == 0:
-                rows = jnp.where(f < live_frames(counts, 0), rows, 0.0)
-            edges_out(rows, even, near, far, start + f)
+            edges_out(source[f].astype(F32), even, near, far, start + f)
+    frames = [second[f].astype(F32) for f in range(2)]
+    upper, lower = ([rows_out(rows, at) for rows in frames] for at in (0, 6))
+    upper = merged(upper[0], rolled(upper[1], 1, 0))
+    lower = merged(rolled(lower[0], -1, 0), lower[1])
+    hand_out(upper, lower, even, near, far, 6)
 
 
 WINDOW = (FRAMES + 2, MAIN, C)
@@ -368,7 +376,7 @@
 def prepare_kernel(r):
     pairs = [(r[n + "_hbm"], r[n]) for n in ("x", "gain1", "bias1", "gain2", "bias2", "second", "incoming")]
     pairs += [(r["counts_hbm"], r["counts"]), (r["first_hbm"], r["window1"].at[pl.ds(0, 2)])]
-    pairs += [(r["weights1_hbm"].at[a], r["weights1"].at[a]) for a in range(3)]
+    pairs += [(r["weights1_hbm"].at[a], r["weights1"].at[a]) for a in range(2)]
     copies = [pltpu.make_async_copy(source, target, r["sems"].at[i]) for i, (source, target) in enumerate(pairs)]
     for copy in copies:
         copy.start()
@@ -387,7 +395,9 @@
 def tick0_kernel(r):
     counting = pltpu.make_async_copy(r["counts_hbm"], r["counts"], r["sems"].at[3])
     counting.start()
-    copies = [pltpu.make_async_copy(r["weights2_hbm"].at[a], r["weights2"].at[a], r["sems"].at[a]) for a in range(3)]
+    pairs = [(r["weights1_hbm"].at[2], r["weights1_last"])]
+    pairs += [(r["weights2_hbm"].at[a], r["weights2"].at[a]) for a in range(3)]
+    copies = [pltpu.make_async_copy(source, target, r["sems"].at[4 + i]) for i, (source, target) in enumerate(pairs)]
     for copy in copies:
         copy.start()
 
@@ -398,7 +408,9 @@
         work.window2[0:2] = work.second[...]
         for g in range(2):
             work.halos[g] = jnp.concatenate(work.halo(4 + g), axis=0).astype(BF16)
-            work.hidden_edges[g] = edge_pair(*work.halo(6 + g))
+        top, bottom = work.halo(6)
+        work.hidden_edges[0] = merged(top, rolled(bottom, 1, 0))
+        work.hidden_edges[1] = merged(rolled(top, -1, 0), bottom)
         last = lax.axis_index("segment") == lax.axis_size("segment") - 1
 
         def finish(f):
@@ -412,17 +424,17 @@
         finishing = [lambda f=f: finish(f) for f in range(FRAMES)]
         phases = [work.phase(conv, pair) for conv in range(2) for pair in (0, 2, 4)]
         groups = [
-            (None, (0, 0), work.first_thunks(0, cached=True)),
             (None, (0, 2), work.first_thunks(2)),
             ((0, 0), (0, 4), work.first_thunks(4)),
             ((0, 0), (0, 4), work.second_thunks(0, cached=True)),
-            ((0, 0), (0, 4), [counting.wait]),
-            ((0, 2), (1, 0), [copy.wait for copy in copies]),
+            ((0, 0), (0, 4), [copies[0].wait]),
+            ((0, 2), (1, 0), [copy.wait for copy in copies[1:]]),
             ((0, 2), (1, 0), work.second_thunks(2)),
             ((0, 4), (1, 2), work.second_thunks(4)),
             ((1, 2), None, finishing[:2]),
         ]
-        work.run(timeline(phases, groups) + finishing[2:])
+        order = work.first_thunks(0, cached=True) + [counting.wait] + timeline(phases, groups)
+        work.run(order + finishing[2:])
 
     with_section(r, body)
 
@@ -578,14 +590,14 @@
     second = flat(second_cache[0])
     near, far = pl.pallas_call(
         pack_kernel,
-        out_shape=[pltpu.VMEM((8, EDGE, C), BF16)] * 2,
-        in_specs=[HBM] + [VMEM] * 3,
+        out_shape=[pltpu.VMEM((7, EDGE, C), BF16)] * 2,
+        in_specs=[VMEM] * 3,
         out_specs=[VMEM] * 2,
-        scratch_shapes=[pltpu.SMEM((9,), jnp.int32), pltpu.SemaphoreType.DMA],
         compiler_params=pltpu.CompilerParams(vmem_limit_bytes=8 << 20),
         name="pack",
-    )(*(pltpu.with_memory_space_constraint(rows, pltpu.HBM) for rows in (frame_counts, x, first, second)))
-    near, far = swap(near, False, 0), swap(far, True, 0)
+    )(*(pltpu.with_memory_space_constraint(rows, pltpu.HBM) for rows in (x, first, second)))
+    far = swap(far, True, 0)
+    near = swap(near, False, 0)
     counts = dict(counts_hbm=frame_counts)
     count_scratch = dict(counts=pltpu.SMEM((9,), jnp.int32), sems=pltpu.SemaphoreType.DMA((16,)))
     block = pltpu.VMEM((FRAMES, MAIN, C), BF16)
@@ -610,17 +622,25 @@
             second=cached,
             incoming=block,
             window1=pltpu.VMEM(WINDOW, BF16),
-            weights1=weights,
+            weights1=pltpu.VMEM((2, K, C), BF16),
             **{n: pltpu.VMEM((1, C), F32) for n in VECTORS},
         ),
         count_scratch,
-        moved=2 * 3 * K * C,
+        moved=2 * 2 * K * C,
     )
     vectors = {n: ready[n] for n in VECTORS}
     done = call(
         tick0_kernel,
-        dict(**counts, near=near, far=far, weights2_hbm=second_kernel[0].reshape(3, K, C), **ready),
         dict(
+            **counts,
+            far=far,
+            near=near,
+            weights1_hbm=first_kernel[0].reshape(3, K, C),
+            weights2_hbm=second_kernel[0].reshape(3, K, C),
+            **ready,
+        ),
+        dict(
+            weights1_last=pltpu.VMEM((K, C), BF16),
             weights2=weights,
             halos=pltpu.VMEM((FRAMES + 2, 2 * EDGE, C), BF16),
             window2=pltpu.VMEM(WINDOW, BF16),
@@ -634,9 +654,10 @@
     )
 
     onward = [(s * strips + k, (s + 1) % segments * strips + k) for s in range(segments) for k in range(strips)]
+    far = swap(done["send_far"], True, 1)
+    near = swap(done["send_near"], False, 1)
     x = lax.ppermute(done["send"], axes, onward)
-    near, far = swap(done["send_near"], False, 1), swap(done["send_far"], True, 1)
-    both = dict(weights1=ready["weights1"], weights2=done["weights2"])
+    both = dict(weights1=ready["weights1"], **{n: done[n] for n in ("weights1_last", "weights2")})
     early = call(
         between_kernel,
         dict(
@@ -667,7 +688,7 @@
         early[name] = early.pop(sums)
     out = call(
         tick1_kernel,
-        dict(**counts, x=x, near=near, far=far, **early, **both, **vectors, base=whole),
+        dict(**counts, far=far, near=near, x=x, **early, **both, **vectors, base=whole),
         dict(whole=shape(2, FRAMES, MAIN, C), first_next=shape(2, MAIN, C), second_next=shape(2, MAIN, C)),
         dict(
             window1=pltpu.VMEM(WINDOW, BF16),

time: 40.1 us -> 38.5 us (0.960)
  Pallas kernels: 27.2 us -> 26.4 us
  waiting for transfers between devices: 5.06 us -> 4.29 us
    ppermute x4, waiting for transfers between devices: 5.06 us -> 4.29 us  [swap(): return lax.ppermute(rows, axes, pairs)]
    pallas_call x1, Pallas kernels: 1.87 us -> 1.27 us  [on_device(): pl.pallas_call(pack_kernel, out_shape=[pltpu.VMEM((7, EDGE, C), BF16)] *...]
  transfers between devices with their start and end apart: 5 -> 5, of which waited for: 2 -> 3; matrix products, arithmetic and copies ran while one was open for 0% -> 0% of each run, Pallas kernels for 19% -> 18%
where the time goes in v5:
time: 38.5 us; the launch traced here: 38.3 us
  Pallas kernels  26.4 us (69%)
  starting transfers between devices  6.81 us (18%)
  waiting for transfers between devices  4.29 us (11%)
  between operations  0.83 us (2%)
    pallas_call x4, Pallas kernels, call(): pl.pallas_call(lambda *refs: kernel(dict(zip(names, refs))), out_shape=li...  25.1 us
    ppermute x4, starting transfers between devices, swap(): return lax.ppermute(rows, axes, pairs)  6.79 us
    ppermute x4, waiting for transfers between devices, swap(): return lax.ppermute(rows, axes, pairs)  4.29 us
    pallas_call x1, Pallas kernels, on_device(): pl.pallas_call(pack_kernel, out_shape=[pltpu.VMEM((7, EDGE, C), BF16)] *...  1.27 us
  transfers between devices with their start and end apart: 5, of which 3 were waited for; matrix products, arithmetic and copies ran while one was open for 0% of the time, Pallas kernels for 18%

profile of v5, /device:TPU:96, one launch (start us, length us, event | category | flops | bytes accessed | tf_op | source)
XLA Modules:
  0.0 38.3 jit_solution(13843852233017385509)
XLA Ops:
  0.6 1.3 %pack.1 = (bf16[7,24,384]{2,1,0:T(8,128)(2,1)S(1)}, bf16[7,24,384]{2,1,0:T(8,128)(2,1)S(1)}) custom-call(bf16[4,96,384]{2,1,0:T(8,128)(2,1)} %bitcast.40, bf16[2,96,384]{2,1,0:T(8,128)(2,1)} %bitcast.43, bf16[2,96,384]{2,1,0:T(8,128)(2,1)} %bitcast.45), custom_call_target="tpu_custom_call" | custom-call | tf_op jit(solution)/shard_map/pack/pallas_call | solution.py:591
  1.9 2.9 %collective-permute-start = (bf16[7,24,384]{2,1,0:T(8,128)(2,1)S(1)}, bf16[7,24,384]{2,1,0:T(8,128)(2,1)S(1)}, u32[]{:S(2)}, u32[]{:S(2)}) collective-permute-start(bf16[7,24,384]{2,1,0:T(8,128)(2,1)S(1)} %get-tuple-element.34), channel_id=1, source_target_pairs={{0,16},{1,2},{2,1},{3,4},{4,3},{5,6},{6,5},{7,8},{8,7},{9,10},{10,... | collective-permute-start | bytes 387080 | tf_op jit(solution)/shard_map/ppermute | solution.py:586
  4.8 0.3 collective-permute-start.1
  5.1 3.1 %prepare.1 = (bf16[4,96,384]{2,1,0:T(8,128)(2,1)S(1)}, bf16[2,96,384]{2,1,0:T(8,128)(2,1)S(1)}, bf16[4,96,384]{2,1,0:T(8,128)(2,1)S(1)}, bf16[6,96,384]{2,1,0:T(...) custom-call(bf16[4,96,384]{2,1,0:T(8,128)(2,1)} %bitcast.41, ...), custom_call_target="tpu_custom_call" | custom-call | bytes 5308416 | tf_op jit(solution)/shard_map/prepare/pallas_call | solution.py:533
  8.2 1.1 %collective-permute-done.refs_1_ = bf16[7,24,384]{2,1,0:T(8,128)(2,1)S(1)} collective-permute-done((bf16[7,24,384]{2,1,0:T(8,128)(2,1)S(1)}, bf16[7,24,384]{2,1,0:T(8,128)(2,1)S(1)}, u32[]{:S(2)}, u32[]{:S(2)}) %collective-permute-start) | collective-permute-done | bytes 129056 | tf_op jit(solution)/shard_map/ppermute | solution.py:586
  9.3 0.5 %collective-permute-done.1.refs_2_ = bf16[7,24,384]{2,1,0:T(8,128)(2,1)S(1)} collective-permute-done((bf16[7,24,384]{2,1,0:T(8,128)(2,1)S(1)}, bf16[7,24,384]{2,1,0:T(8,128)(2,1)S(1)}, u32[]{:S(2)}, u32[]{:S(2)}) %collective-permute-start.1) | collective-permute-done | bytes 129056 | tf_op jit(solution)/shard_map/ppermute | solution.py:586
  9.8 9.9 %tick0.1 = (bf16[3456,384]{1,0:T(8,128)(2,1)S(1)}, bf16[3,3456,384]{2,1,0:T(8,128)(2,1)S(1)}, bf16[6,48,384]{2,1,0:T(8,128)(2,1)S(1)}, bf16[6,96,384]{2,1,0:T(8,...) custom-call(s32[9]{0:T(128)} %refs_0_.5, ...), custom_call_target="tpu_custom_call" | custom-call | tf_op jit(solution)/shard_map/tick0/pallas_call | solution.py:533
  19.7 0.0 collective-permute-start.4
  19.7 3.6 %collective-permute-start.2 = (bf16[4,24,384]{2,1,0:T(8,128)(2,1)S(1)}, bf16[4,24,384]{2,1,0:T(8,128)(2,1)S(1)}, u32[]{:S(2)}, u32[]{:S(2)}) collective-permute-start(bf16[4,24,384]{2,1,0:T(8,128)(2,1)S(1)} %get-tuple-element.45), channel_id=1, source_target_pairs={{0,16},{1,18},{2,17},{3,20},{4,19},{5,22},{6,21},{7,24},{8,23},{9,... | collective-permute-start | bytes 221192 | tf_op jit(solution)/shard_map/ppermute | solution.py:586
  23.3 0.0 collective-permute-start.3
  23.3 3.6 %between.1 = (bf16[2,4,96,384]{3,2,1,0:T(8,128)(2,1)}, bf16[2,96,384]{2,1,0:T(8,128)(2,1)S(1)}, bf16[2,48,384]{2,1,0:T(8,128)(2,1)S(1)}, bf16[2,96,384]{2,1,0:T(...) custom-call(s32[9]{0:T(128)} %refs_0_.5, ...), custom_call_target="tpu_custom_call" | custom-call | flops 1528823808 | bytes 7962624 | tf_op jit(solution)/shard_map/between/pallas_call | solution.py:533
  26.9 2.7 %collective-permute-done.2.refs_1_ = bf16[4,24,384]{2,1,0:T(8,128)(2,1)S(1)} collective-permute-done((bf16[4,24,384]{2,1,0:T(8,128)(2,1)S(1)}, bf16[4,24,384]{2,1,0:T(8,128)(2,1)S(1)}, u32[]{:S(2)}, u32[]{:S(2)}) %collective-permute-start.2) | collective-permute-done | bytes 73760 | tf_op jit(solution)/shard_map/ppermute | solution.py:586
  29.7 0.0 collective-permute-done.3.refs_2_
  29.7 0.0 collective-permute-done.4.refs_3_
  29.7 8.5 %tick1.1 = (bf16[2,4,96,384]{3,2,1,0:T(8,128)(2,1)}, bf16[2,96,384]{2,1,0:T(8,128)(2,1)}, bf16[2,96,384]{2,1,0:T(8,128)(2,1)}) custom-call(s32[9]{0:T(128)} %refs_0_.5, bf16[4,24,384]{2,1,0:T(8,128)(2,1)S(1)} %collective-permute-done.2.refs_1_, bf16[4,24,384]{2,1,0:T(8,128)(2,1)S(1)} %collective-permute-done.3.refs_2_, ...), custom_call_target="tpu_custom_call", output_to_operand_aliasing={{0}: (18, {})} | custom-call | tf_op jit(solution)/shard_map/tick1/pallas_call | solution.py:533
Async XLA Ops:
  1.9 7.4 %collective-permute-start = (bf16[7,24,384]{2,1,0:T(8,128)(2,1)S(1)}, bf16[7,24,384]{2,1,0:T(8,128)(2,1)S(1)}, u32[]{:S(2)}, u32[]{:S(2)}) collective-permute-start(bf16[7,24,384]{2,1,0:T(8,128)(2,1)S(1)} %get-tuple-element.34), channel_id=1, source_target_pairs={{0,16},{1,2},{2,1},{3,4},{4,3},{5,6},{6,5},{7,8},{8,7},{9,10},{10,... | collective-permute-start | bytes 387080 | tf_op jit(solution)/shard_map/ppermute | solution.py:586
  4.8 4.9 %collective-permute-start.1 = (bf16[7,24,384]{2,1,0:T(8,128)(2,1)S(1)}, bf16[7,24,384]{2,1,0:T(8,128)(2,1)S(1)}, u32[]{:S(2)}, u32[]{:S(2)}) collective-permute-start(bf16[7,24,384]{2,1,0:T(8,128)(2,1)S(1)} %get-tuple-element.35), channel_id=1, source_target_pairs={{0,1},{1,0},{2,3},{3,2},{4,5},{5,4},{6,7},{7,6},{8,9},{9,8},{10,11... | collective-permute-start | bytes 387080 | tf_op jit(solution)/shard_map/ppermute | solution.py:586
  19.7 10.0 %collective-permute-start.4 = (bf16[4,96,384]{2,1,0:T(8,128)(2,1)S(1)}, bf16[4,96,384]{2,1,0:T(8,128)(2,1)S(1)}, u32[]{:S(2)}, u32[]{:S(2)}) collective-permute-start(bf16[4,96,384]{2,1,0:T(8,128)(2,1)S(1)} %get-tuple-element.47), channel_id=1, source_target_pairs={{0,16},{1,17},{2,18},{3,19},{4,20},{5,21},{6,22},{7,23},{8,24},{9,... | collective-permute-start | bytes 884744 | tf_op jit(solution)/shard_map/ppermute | solution.py:659
  19.7 9.9 %collective-permute-start.2 = (bf16[4,24,384]{2,1,0:T(8,128)(2,1)S(1)}, bf16[4,24,384]{2,1,0:T(8,128)(2,1)S(1)}, u32[]{:S(2)}, u32[]{:S(2)}) collective-permute-start(bf16[4,24,384]{2,1,0:T(8,128)(2,1)S(1)} %get-tuple-element.45), channel_id=1, source_target_pairs={{0,16},{1,18},{2,17},{3,20},{4,19},{5,22},{6,21},{7,24},{8,23},{9,... | collective-permute-start | bytes 221192 | tf_op jit(solution)/shard_map/ppermute | solution.py:586
  23.3 6.4 %collective-permute-start.3 = (bf16[4,24,384]{2,1,0:T(8,128)(2,1)S(1)}, bf16[4,24,384]{2,1,0:T(8,128)(2,1)S(1)}, u32[]{:S(2)}, u32[]{:S(2)}) collective-permute-start(bf16[4,24,384]{2,1,0:T(8,128)(2,1)S(1)} %get-tuple-element.46), channel_id=1, source_target_pairs={{0,17},{1,16},{2,19},{3,18},{4,21},{5,20},{6,23},{7,22},{8,25},{9,... | collective-permute-start | bytes 221192 | tf_op jit(solution)/shard_map/ppermute | solution.py:586

commit v6 on v5

--- a/solution.py
+++ b/solution.py
@@ -126,7 +126,7 @@
                 clock[unit] += sum(operand.shape[1] for _, operand, _ in step[4])
             ends[name, unit] = clock[unit]
     for after, before, thunks in groups:
-        first = max(ends[after, 0], ends[after, 1]) if after else -1
+        first = max(ends[after, 0], ends[after, 1]) if isinstance(after, tuple) else after
         last = min(starts[before, 0], starts[before, 1]) if before else max(clock) + 1
         last = max(last, first + 0.5)
         for i, thunk in enumerate(thunks):
@@ -424,7 +424,7 @@
         finishing = [lambda f=f: finish(f) for f in range(FRAMES)]
         phases = [work.phase(conv, pair) for conv in range(2) for pair in (0, 2, 4)]
         groups = [
-            (None, (0, 2), work.first_thunks(2)),
+            (1280, (0, 2), [counting.wait] + work.first_thunks(2)),
             ((0, 0), (0, 4), work.first_thunks(4)),
             ((0, 0), (0, 4), work.second_thunks(0, cached=True)),
             ((0, 0), (0, 4), [copies[0].wait]),
@@ -433,7 +433,7 @@
             ((0, 4), (1, 2), work.second_thunks(4)),
             ((1, 2), None, finishing[:2]),
         ]
-        order = work.first_thunks(0, cached=True) + [counting.wait] + timeline(phases, groups)
+        order = work.first_thunks(0, cached=True) + timeline(phases, groups)
         work.run(order + finishing[2:])
 
     with_section(r, body)
@@ -467,7 +467,7 @@
                 work.sum_edges[:, TILE:C] = halves(work.right_edges[0])[0]
 
         order = work.first_thunks(0, cached=True)
-        order += timeline([work.phase(0, 0)], [(None, None, work.second_thunks(0, cached=True))])
+        order += timeline([work.phase(0, 0)], [(-1, None, work.second_thunks(0, cached=True))])
         order += [lambda: store(0, work.sum1)]
         order += timeline([work.phase(1, 0)], [])
         work.run(order)
@@ -489,7 +489,7 @@
 
     def body(work):
         work.norms = True
-        work.moved = (1,)
+        work.moved = (0,)
         work.live = lambda: live_frames(r["counts"], 1)
         for i in range(2):
             work.window1[i] = work.first[i]
@@ -507,8 +507,8 @@
         finishing = [lambda f=f: finish(f) for f in range(FRAMES)]
         phases = [work.phase(conv, pair) for conv in range(2) for pair in (2, 4)]
         groups = [
-            (None, (0, 4), work.first_thunks(4)),
-            (None, (0, 4), [counting.wait]),
+            (-1, (0, 4), work.first_thunks(4)),
+            (-1, (0, 4), [counting.wait]),
             ((0, 2), (1, 2), work.second_thunks(2)),
             ((0, 2), (1, 2), [lambda: send_window(work.window1, work.first_next)]),
             ((0, 4), (1, 4), work.second_thunks(4)),

time: 38.5 us -> 38.2 us (level)
  no operation moved by 1% of the time
where the time goes in v6:
time: 38.2 us; the launch traced here: 38.1 us
  Pallas kernels  26.1 us (68%)
  starting transfers between devices  6.81 us (18%)
  waiting for transfers between devices  4.3 us (11%)
  between operations  0.83 us (2%)
    pallas_call x4, Pallas kernels, call(): pl.pallas_call(lambda *refs: kernel(dict(zip(names, refs))), out_shape=li...  24.9 us
    ppermute x4, starting transfers between devices, swap(): return lax.ppermute(rows, axes, pairs)  6.79 us
    ppermute x4, waiting for transfers between devices, swap(): return lax.ppermute(rows, axes, pairs)  4.29 us
    pallas_call x1, Pallas kernels, on_device(): pl.pallas_call(pack_kernel, out_shape=[pltpu.VMEM((7, EDGE, C), BF16)] *...  1.27 us
  transfers between devices with their start and end apart: 5, of which 3 were waited for; matrix products, arithmetic and copies ran while one was open for 0% of the time, Pallas kernels for 18%

profile of v6, /device:TPU:96, one launch (start us, length us, event | category | flops | bytes accessed | tf_op | source)
XLA Modules:
  0.0 38.1 jit_solution(14502916228360710121)
XLA Ops:
  0.6 1.3 %pack.1 = (bf16[7,24,384]{2,1,0:T(8,128)(2,1)S(1)}, bf16[7,24,384]{2,1,0:T(8,128)(2,1)S(1)}) custom-call(bf16[4,96,384]{2,1,0:T(8,128)(2,1)} %bitcast.40, bf16[2,96,384]{2,1,0:T(8,128)(2,1)} %bitcast.43, bf16[2,96,384]{2,1,0:T(8,128)(2,1)} %bitcast.45), custom_call_target="tpu_custom_call" | custom-call | tf_op jit(solution)/shard_map/pack/pallas_call | solution.py:591
  1.9 2.9 %collective-permute-start = (bf16[7,24,384]{2,1,0:T(8,128)(2,1)S(1)}, bf16[7,24,384]{2,1,0:T(8,128)(2,1)S(1)}, u32[]{:S(2)}, u32[]{:S(2)}) collective-permute-start(bf16[7,24,384]{2,1,0:T(8,128)(2,1)S(1)} %get-tuple-element.34), channel_id=1, source_target_pairs={{0,16},{1,2},{2,1},{3,4},{4,3},{5,6},{6,5},{7,8},{8,7},{9,10},{10,... | collective-permute-start | bytes 387080 | tf_op jit(solution)/shard_map/ppermute | solution.py:586
  4.8 0.3 collective-permute-start.1
  5.1 3.1 %prepare.1 = (bf16[4,96,384]{2,1,0:T(8,128)(2,1)S(1)}, bf16[2,96,384]{2,1,0:T(8,128)(2,1)S(1)}, bf16[4,96,384]{2,1,0:T(8,128)(2,1)S(1)}, bf16[6,96,384]{2,1,0:T(...) custom-call(bf16[4,96,384]{2,1,0:T(8,128)(2,1)} %bitcast.41, ...), custom_call_target="tpu_custom_call" | custom-call | bytes 5308416 | tf_op jit(solution)/shard_map/prepare/pallas_call | solution.py:533
  8.2 1.1 %collective-permute-done.refs_1_ = bf16[7,24,384]{2,1,0:T(8,128)(2,1)S(1)} collective-permute-done((bf16[7,24,384]{2,1,0:T(8,128)(2,1)S(1)}, bf16[7,24,384]{2,1,0:T(8,128)(2,1)S(1)}, u32[]{:S(2)}, u32[]{:S(2)}) %collective-permute-start) | collective-permute-done | bytes 129056 | tf_op jit(solution)/shard_map/ppermute | solution.py:586
  9.3 0.5 %collective-permute-done.1.refs_2_ = bf16[7,24,384]{2,1,0:T(8,128)(2,1)S(1)} collective-permute-done((bf16[7,24,384]{2,1,0:T(8,128)(2,1)S(1)}, bf16[7,24,384]{2,1,0:T(8,128)(2,1)S(1)}, u32[]{:S(2)}, u32[]{:S(2)}) %collective-permute-start.1) | collective-permute-done | bytes 129056 | tf_op jit(solution)/shard_map/ppermute | solution.py:586
  9.8 9.8 %tick0.1 = (bf16[3456,384]{1,0:T(8,128)(2,1)S(1)}, bf16[3,3456,384]{2,1,0:T(8,128)(2,1)S(1)}, bf16[6,48,384]{2,1,0:T(8,128)(2,1)S(1)}, bf16[6,96,384]{2,1,0:T(8,...) custom-call(s32[9]{0:T(128)} %refs_0_.5, ...), custom_call_target="tpu_custom_call" | custom-call | tf_op jit(solution)/shard_map/tick0/pallas_call | solution.py:533
  19.6 0.0 collective-permute-start.4
  19.6 3.6 %collective-permute-start.2 = (bf16[4,24,384]{2,1,0:T(8,128)(2,1)S(1)}, bf16[4,24,384]{2,1,0:T(8,128)(2,1)S(1)}, u32[]{:S(2)}, u32[]{:S(2)}) collective-permute-start(bf16[4,24,384]{2,1,0:T(8,128)(2,1)S(1)} %get-tuple-element.45), channel_id=1, source_target_pairs={{0,16},{1,18},{2,17},{3,20},{4,19},{5,22},{6,21},{7,24},{8,23},{9,... | collective-permute-start | bytes 221192 | tf_op jit(solution)/shard_map/ppermute | solution.py:586
  23.2 0.0 collective-permute-start.3
  23.2 3.6 %between.1 = (bf16[2,4,96,384]{3,2,1,0:T(8,128)(2,1)}, bf16[2,96,384]{2,1,0:T(8,128)(2,1)S(1)}, bf16[2,48,384]{2,1,0:T(8,128)(2,1)S(1)}, bf16[2,96,384]{2,1,0:T(...) custom-call(s32[9]{0:T(128)} %refs_0_.5, ...), custom_call_target="tpu_custom_call" | custom-call | flops 1528823808 | bytes 7962624 | tf_op jit(solution)/shard_map/between/pallas_call | solution.py:533
  26.9 2.7 %collective-permute-done.2.refs_1_ = bf16[4,24,384]{2,1,0:T(8,128)(2,1)S(1)} collective-permute-done((bf16[4,24,384]{2,1,0:T(8,128)(2,1)S(1)}, bf16[4,24,384]{2,1,0:T(8,128)(2,1)S(1)}, u32[]{:S(2)}, u32[]{:S(2)}) %collective-permute-start.2) | collective-permute-done | bytes 73760 | tf_op jit(solution)/shard_map/ppermute | solution.py:586
  29.6 0.0 collective-permute-done.3.refs_2_
  29.6 0.0 collective-permute-done.4.refs_3_
  29.6 8.3 %tick1.1 = (bf16[2,4,96,384]{3,2,1,0:T(8,128)(2,1)}, bf16[2,96,384]{2,1,0:T(8,128)(2,1)}, bf16[2,96,384]{2,1,0:T(8,128)(2,1)}) custom-call(s32[9]{0:T(128)} %refs_0_.5, bf16[4,24,384]{2,1,0:T(8,128)(2,1)S(1)} %collective-permute-done.2.refs_1_, bf16[4,24,384]{2,1,0:T(8,128)(2,1)S(1)} %collective-permute-done.3.refs_2_, ...), custom_call_target="tpu_custom_call", output_to_operand_aliasing={{0}: (18, {})} | custom-call | tf_op jit(solution)/shard_map/tick1/pallas_call | solution.py:533
Async XLA Ops:
  1.9 7.4 %collective-permute-start = (bf16[7,24,384]{2,1,0:T(8,128)(2,1)S(1)}, bf16[7,24,384]{2,1,0:T(8,128)(2,1)S(1)}, u32[]{:S(2)}, u32[]{:S(2)}) collective-permute-start(bf16[7,24,384]{2,1,0:T(8,128)(2,1)S(1)} %get-tuple-element.34), channel_id=1, source_target_pairs={{0,16},{1,2},{2,1},{3,4},{4,3},{5,6},{6,5},{7,8},{8,7},{9,10},{10,... | collective-permute-start | bytes 387080 | tf_op jit(solution)/shard_map/ppermute | solution.py:586
  4.8 4.9 %collective-permute-start.1 = (bf16[7,24,384]{2,1,0:T(8,128)(2,1)S(1)}, bf16[7,24,384]{2,1,0:T(8,128)(2,1)S(1)}, u32[]{:S(2)}, u32[]{:S(2)}) collective-permute-start(bf16[7,24,384]{2,1,0:T(8,128)(2,1)S(1)} %get-tuple-element.35), channel_id=1, source_target_pairs={{0,1},{1,0},{2,3},{3,2},{4,5},{5,4},{6,7},{7,6},{8,9},{9,8},{10,11... | collective-permute-start | bytes 387080 | tf_op jit(solution)/shard_map/ppermute | solution.py:586
  19.6 10.0 %collective-permute-start.4 = (bf16[4,96,384]{2,1,0:T(8,128)(2,1)S(1)}, bf16[4,96,384]{2,1,0:T(8,128)(2,1)S(1)}, u32[]{:S(2)}, u32[]{:S(2)}) collective-permute-start(bf16[4,96,384]{2,1,0:T(8,128)(2,1)S(1)} %get-tuple-element.47), channel_id=1, source_target_pairs={{0,16},{1,17},{2,18},{3,19},{4,20},{5,21},{6,22},{7,23},{8,24},{9,... | collective-permute-start | bytes 884744 | tf_op jit(solution)/shard_map/ppermute | solution.py:659
  19.6 9.9 %collective-permute-start.2 = (bf16[4,24,384]{2,1,0:T(8,128)(2,1)S(1)}, bf16[4,24,384]{2,1,0:T(8,128)(2,1)S(1)}, u32[]{:S(2)}, u32[]{:S(2)}) collective-permute-start(bf16[4,24,384]{2,1,0:T(8,128)(2,1)S(1)} %get-tuple-element.45), channel_id=1, source_target_pairs={{0,16},{1,18},{2,17},{3,20},{4,19},{5,22},{6,21},{7,24},{8,23},{9,... | collective-permute-start | bytes 221192 | tf_op jit(solution)/shard_map/ppermute | solution.py:586
  23.2 6.4 %collective-permute-start.3 = (bf16[4,24,384]{2,1,0:T(8,128)(2,1)S(1)}, bf16[4,24,384]{2,1,0:T(8,128)(2,1)S(1)}, u32[]{:S(2)}, u32[]{:S(2)}) collective-permute-start(bf16[4,24,384]{2,1,0:T(8,128)(2,1)S(1)} %get-tuple-element.46), channel_id=1, source_target_pairs={{0,17},{1,16},{2,19},{3,18},{4,21},{5,20},{6,23},{7,22},{8,25},{9,... | collective-permute-start | bytes 221192 | tf_op jit(solution)/shard_map/ppermute | solution.py:586
